TPU v7x, 256 devices: a whole 4x4x8 slice. The times are simulated.
256 devices in a mesh: seq: 64 (over y, x, z_hi, core), fs: 4 (over z_lo).
Axes of the slice: x: 4, y: 4, z: 8 (z_hi: 2, z_lo: 4; z = z_hi * 4 + z_lo), core: 2. Of those that a mesh axis runs over, the one named last changes fastest.
Arguments:
- hidden: bfloat16 [16384, 8192], P(('seq', 'fs')), may hold values from -6 to 6
- norm_gain: bfloat16 [8192], replicated, may hold values from 0.099609375 to 1.8984375
- kv_weight: bfloat16 [8192, 1024], P('seq', 'fs'), may hold values from -0.0625 to 0.0625
- queries: bfloat16 [16384, 4096], P('seq', 'fs'), may hold values from -136 to 136
- segment_ids: int32 [16384], P('seq'), may hold values from 0 to 3, never falling along the last dimension, each value on 1 to 8192 neighbouring positions
- page_owner: int32 [4096, 1], P('seq'), may hold values from 0 to 63; in each aligned block of 64 rows (0 to 63, 64 to 127, ...) at most 2 rows name the same one
Outputs:
- attended: bfloat16 [16384, 4096], P('seq', 'fs')
- kv_cache: bfloat16 [64, 64, 2, 4, 1024], P('seq', None, None, None, 'fs')
Inputs may be any that keep to these rules, and one draw needn't show every extreme that they name: `segment_ids`: prompt ids never fall along the stream; each of the 4 prompts holds 1 to 8192 tokens and one holds exactly 8192. `page_owner`: among the 64 pages of one block no owner is named more than 2 times, a bound that some block reaches.
All inputs are finite; a program needn't handle non-finite values.
Results may differ from a plain program's by a relative error of at most 0.01.
The roundings to bfloat16 on the way count: a program that leaves them out, or rounds other values in their place, can miss the bound.
Values may be sent and summed in bfloat16 or wider, within the bound.
A program may use at most 64 MiB of HBM per device.

v0:
```python
import jax
import jax.numpy as jnp
from jax import lax
from jax.sharding import PartitionSpec as P

HD = 128
SEGS = 4


EPSILON = 1e-05
NEGATIVE = -1e30


def shifted(value, axis, steps):
    count = lax.axis_size(axis)
    initial, last = (max(0, -steps), min(count, count - steps))
    return lax.ppermute(value, axis, [(source, source + steps) for source in range(initial, last)])


def rotate_keys(keys, positions):
    half = keys.shape[-1] // 2
    freq = 10000.0 ** (-jnp.arange(half, dtype=jnp.float32) * 2.0 / keys.shape[-1])
    angle = positions.astype(jnp.float32)[:, None] * freq[None, :]
    cosine = jnp.cos(angle)[:, None, :]
    sine = jnp.sin(angle)[:, None, :]
    first = keys[..., :half]
    second = keys[..., half:]
    return jnp.concatenate(
        [first * cosine - second * sine, second * cosine + first * sine], axis=-1
    )


def pair_keys(projected, positions, head_size):
    rows = projected.shape[0]
    pairs = projected.reshape(rows, -1, 2, head_size)
    turned = rotate_keys(pairs[:, :, 0], positions)
    return jnp.stack([turned, pairs[:, :, 1]], axis=2).reshape(rows, -1).astype(jnp.bfloat16)


def on_device(hidden, norm_gain, kv_weight, queries, segment_ids, page_owner):
    seq_count = lax.axis_size("seq")
    seq_place = lax.axis_index("seq")
    block_rows = segment_ids.shape[0]
    stream_rows = block_rows * seq_count
    prompt_count = SEGS
    anchor = seq_place * block_rows
    token_index = anchor + jnp.arange(block_rows, dtype=jnp.int32)
    labels = jnp.arange(prompt_count, dtype=jnp.int32)
    member = segment_ids[:, None] == labels[None, :]
    firsts = jnp.min(jnp.where(member, token_index[:, None], stream_rows), axis=0)
    starts = lax.pmin(firsts, "seq")
    query_start = jnp.sum(jnp.where(member, starts[None, :], 0), axis=1)
    positions = token_index - query_start
    wide = hidden.astype(jnp.float32)
    stat = jnp.mean(wide * wide, axis=1, keepdims=True)
    normed = (wide * lax.rsqrt(stat + EPSILON) * norm_gain.astype(jnp.float32)[None, :]).astype(
        jnp.bfloat16
    )
    gathered = lax.all_gather(normed, "fs", axis=0, tiled=True)
    projected = jnp.dot(
        gathered,
        lax.all_gather(kv_weight, "seq", axis=0, tiled=True),
        preferred_element_type=jnp.float32,
    )
    kv_block = pair_keys(projected, positions, HD)
    head_count = queries.shape[1] // HD
    kv_heads = kv_block.shape[1] // (2 * HD)
    group = head_count // kv_heads
    scale = HD ** (-0.5)
    query_heads = queries.reshape(block_rows, kv_heads, group, HD)

    def attend(state, pairs, source_block):
        running_max, totals, summed = state
        pairs_four = pairs.reshape(block_rows, kv_heads, 2, HD)
        keys = pairs_four[:, :, 0]
        values = pairs_four[:, :, 1]
        scores = (
            jnp.einsum("qhgd,khd->hgqk", query_heads, keys, preferred_element_type=jnp.float32)
            * scale
        )
        key_index = source_block * block_rows + jnp.arange(block_rows, dtype=jnp.int32)
        allowed = (key_index[None, :] >= query_start[:, None]) & (
            key_index[None, :] <= token_index[:, None]
        )
        scores = jnp.where(allowed[None, None], scores, NEGATIVE)
        new_max = jnp.maximum(running_max, jnp.max(scores, axis=-1))
        weights = jnp.exp(scores - new_max[..., None])
        factor = jnp.exp(running_max - new_max)
        totals = totals * factor + jnp.sum(weights, axis=-1)
        rounded = weights.astype(jnp.bfloat16)
        update = jnp.einsum("hgqk,khd->hgqd", rounded, values, preferred_element_type=jnp.float32)
        summed = summed * factor[..., None] + update
        return (new_max, totals, summed)

    initial = (
        jnp.full((kv_heads, group, block_rows), NEGATIVE, jnp.float32),
        jnp.zeros((kv_heads, group, block_rows), jnp.float32),
        jnp.zeros((kv_heads, group, block_rows, HD), jnp.float32),
    )
    state = attend(initial, kv_block, seq_place)
    longest = stream_rows // 2
    reach = min(seq_count - 1, (longest - 1) // block_rows + 1)

    def one_hop(hop_step, carry):
        travel, inner = carry
        travel = shifted(travel, "seq", 1)
        source_block = seq_place - hop_step
        inner = attend(inner, travel, source_block)
        return (travel, inner)

    travel, state = lax.fori_loop(1, reach + 1, one_hop, (kv_block, state))
    running_max, totals, summed = state
    result = summed / totals[..., None]
    attended = (
        result.transpose(2, 0, 1, 3).reshape(block_rows, head_count * HD).astype(jnp.bfloat16)
    )
    pages_block = page_owner.shape[0]
    page_rows = block_rows // pages_block
    capacity = max(2, 2 * pages_block // seq_count)
    owners = page_owner[:, 0]
    order = jnp.arange(pages_block, dtype=jnp.int32)
    earlier = (owners[None, :] == owners[:, None]) & (order[None, :] < order[:, None])
    rank = jnp.sum(earlier.astype(jnp.int32), axis=1)
    target = owners * capacity + rank
    select = (jnp.arange(seq_count * capacity, dtype=jnp.int32)[:, None] == target[None, :]).astype(
        jnp.bfloat16
    )
    columns_dev = kv_block.shape[1]
    pages = kv_block.reshape(pages_block, page_rows * columns_dev)
    outgoing = jnp.dot(select, pages, preferred_element_type=jnp.float32).astype(jnp.bfloat16)
    outgoing = outgoing.reshape(seq_count, capacity, page_rows, columns_dev)
    arrived = lax.all_to_all(outgoing, "seq", split_axis=0, concat_axis=0, tiled=True)
    kv_cache = arrived.reshape(1, seq_count, capacity, page_rows, columns_dev)
    return (attended, kv_cache)


def solution(mesh):
    placed = (P(("seq", "fs"), None), P(), P("seq", "fs"), P("seq", "fs"), P("seq"), P("seq", None))
    return jax.shard_map(
        on_device,
        mesh=mesh,
        in_specs=placed,
        out_specs=(P("seq", "fs"), P("seq", None, None, None, "fs")),
        check_vma=False,
    )
```

profile of v0, /device:TPU:49, one launch (start us, length us, event | category | flops | bytes accessed | tf_op | source)
XLA Modules:
  0.0 695.7 jit_solution(11367759810542646591)
XLA Ops:
  9.5 2.6 fusion.12
  13.1 18.4 %pmin.7 = s32[4]{0:T(128)S(1)} all-reduce(s32[4]{0:T(128)S(1)} %select_reduce_fusion.1), channel_id=1, replica_groups=mesh['seq'=64,'fs'=4] {'seq'}, use_global_device_ids=true, to_apply=%region_2.3 | all-reduce | flops 4 | bytes 32 | tf_op jit(solution)/shard_map/pmin | solution.py:51
  32.4 66.3 %all-gather.3.cloned.1.call-done = bf16[256,8192]{1,0:T(8,128)(2,1)} async-done(((bf16[64,8192]{1,0:T(8,128)(2,1)}), bf16[256,8192]{1,0:T(8,128)(2,1)}) %all-gather.3.cloned.1.call-update) | async-done | bytes 4194320 | tf_op jit(solution)/shard_map/all_gather | solution.py:59
  98.7 94.5 %all-gather.5.cloned.1.call-done = bf16[8192,256]{1,0:T(8,128)(2,1)} async-done(((bf16[128,256]{1,0:T(8,128)(2,1)}), bf16[8192,256]{1,0:T(8,128)(2,1)}) %all-gather.5.cloned.1.call-update) | async-done | bytes 4194320 | tf_op jit(solution)/shard_map/all_gather | solution.py:62
  193.3 5.2 fusion.33
  202.4 7.5 %all-to-all-start = ((bf16[64,2,4,256]{3,2,1,0:T(4,128)(2,1)}), bf16[64,2,4,256]{3,2,1,0:T(4,128)(2,1)S(1)}, u32[]{:S(2)}, u32[]{:S(2)}) async-start(bf16[64,2,4,256]{3,2,1,0:T(4,128)(2,1)} %reshape.423), calls=%async_computation | async-start | bytes 524288 | tf_op jit(solution)/shard_map/all_to_all | solution.py:132
  209.8 476.7 %while.20 = (s32[]{:T(128)}, bf16[256,256]{0,1:T(8,128)(2,1)S(1)}, f32[1,8,256]{2,1,0:T(8,128)S(1)}, f32[1,8,256]{2,1,0:T(8,128)S(1)}, f32[1,8,256,128]{3,2,1,0:...) while((s32[]{:T(128)}, bf16[256,256]{0,1:T(8,128)(2,1)S(1)}, ...), condition=%wide.region_9.10_spmd.clone, body=%wide.region_6.9_spmd.clone.sunk | while | flops 272833024 | bytes 10097845 | solution.py:111
  209.8 7.3 %collective-permute-start = (bf16[256,256]{0,1:T(8,128)(2,1)S(1)}, bf16[256,256]{0,1:T(8,128)(2,1)S(1)}, u32[]{:S(2)}, u32[]{:S(2)}) collective-permute-start(bf16[256,256]{0,1:T(8,128)(2,1)S(1)} %get-tuple-element.308), channel_id=1, source_target_pairs={{0,4},{4,8},{8,12},{12,16},{16,20},{20,24},{24,28},{28,32},{32,36}... | collective-permute-start | bytes 393224 | tf_op jit(solution)/shard_map/while/body/eval_jaxpr/ppermute | solution.py:17
  220.9 8.3 %collective-permute-start = (bf16[256,256]{0,1:T(8,128)(2,1)S(1)}, bf16[256,256]{0,1:T(8,128)(2,1)S(1)}, u32[]{:S(2)}, u32[]{:S(2)}) collective-permute-start(bf16[256,256]{0,1:T(8,128)(2,1)S(1)} %get-tuple-element.308), channel_id=1, source_target_pairs={{0,4},{4,8},{8,12},{12,16},{16,20},{20,24},{24,28},{28,32},{32,36}... | collective-permute-start | bytes 393224 | tf_op jit(solution)/shard_map/while/body/eval_jaxpr/ppermute | solution.py:17
  233.0 8.3 %collective-permute-start = (bf16[256,256]{0,1:T(8,128)(2,1)S(1)}, bf16[256,256]{0,1:T(8,128)(2,1)S(1)}, u32[]{:S(2)}, u32[]{:S(2)}) collective-permute-start(bf16[256,256]{0,1:T(8,128)(2,1)S(1)} %get-tuple-element.308), channel_id=1, source_target_pairs={{0,4},{4,8},{8,12},{12,16},{16,20},{20,24},{24,28},{28,32},{32,36}... | collective-permute-start | bytes 393224 | tf_op jit(solution)/shard_map/while/body/eval_jaxpr/ppermute | solution.py:17
  241.4 5.4 collective-permute-done
  248.7 4.7 collective-permute-start
  253.6 8.4 %collective-permute-done = bf16[256,256]{0,1:T(8,128)(2,1)S(1)} collective-permute-done((bf16[256,256]{0,1:T(8,128)(2,1)S(1)}, bf16[256,256]{0,1:T(8,128)(2,1)S(1)}, u32[]{:S(2)}, u32[]{:S(2)}) %collective-permute-start) | collective-permute-done | bytes 131104 | tf_op jit(solution)/shard_map/while/body/eval_jaxpr/ppermute | solution.py:17
  266.0 11.2 %collective-permute-done = bf16[256,256]{0,1:T(8,128)(2,1)S(1)} collective-permute-done((bf16[256,256]{0,1:T(8,128)(2,1)S(1)}, bf16[256,256]{0,1:T(8,128)(2,1)S(1)}, u32[]{:S(2)}, u32[]{:S(2)}) %collective-permute-start) | collective-permute-done | bytes 131104 | tf_op jit(solution)/shard_map/while/body/eval_jaxpr/ppermute | solution.py:17
  279.1 1.9 collective-permute-start
  281.1 11.1 %collective-permute-done = bf16[256,256]{0,1:T(8,128)(2,1)S(1)} collective-permute-done((bf16[256,256]{0,1:T(8,128)(2,1)S(1)}, bf16[256,256]{0,1:T(8,128)(2,1)S(1)}, u32[]{:S(2)}, u32[]{:S(2)}) %collective-permute-start) | collective-permute-done | bytes 131104 | tf_op jit(solution)/shard_map/while/body/eval_jaxpr/ppermute | solution.py:17
  296.2 11.1 %collective-permute-done = bf16[256,256]{0,1:T(8,128)(2,1)S(1)} collective-permute-done((bf16[256,256]{0,1:T(8,128)(2,1)S(1)}, bf16[256,256]{0,1:T(8,128)(2,1)S(1)}, u32[]{:S(2)}, u32[]{:S(2)}) %collective-permute-start) | collective-permute-done | bytes 131104 | tf_op jit(solution)/shard_map/while/body/eval_jaxpr/ppermute | solution.py:17
  311.3 11.1 %collective-permute-done = bf16[256,256]{0,1:T(8,128)(2,1)S(1)} collective-permute-done((bf16[256,256]{0,1:T(8,128)(2,1)S(1)}, bf16[256,256]{0,1:T(8,128)(2,1)S(1)}, u32[]{:S(2)}, u32[]{:S(2)}) %collective-permute-start) | collective-permute-done | bytes 131104 | tf_op jit(solution)/shard_map/while/body/eval_jaxpr/ppermute | solution.py:17
  324.3 1.9 collective-permute-start
  326.4 11.1 %collective-permute-done = bf16[256,256]{0,1:T(8,128)(2,1)S(1)} collective-permute-done((bf16[256,256]{0,1:T(8,128)(2,1)S(1)}, bf16[256,256]{0,1:T(8,128)(2,1)S(1)}, u32[]{:S(2)}, u32[]{:S(2)}) %collective-permute-start) | collective-permute-done | bytes 131104 | tf_op jit(solution)/shard_map/while/body/eval_jaxpr/ppermute | solution.py:17
  341.5 11.1 %collective-permute-done = bf16[256,256]{0,1:T(8,128)(2,1)S(1)} collective-permute-done((bf16[256,256]{0,1:T(8,128)(2,1)S(1)}, bf16[256,256]{0,1:T(8,128)(2,1)S(1)}, u32[]{:S(2)}, u32[]{:S(2)}) %collective-permute-start) | collective-permute-done | bytes 131104 | tf_op jit(solution)/shard_map/while/body/eval_jaxpr/ppermute | solution.py:17
  356.6 11.1 %collective-permute-done = bf16[256,256]{0,1:T(8,128)(2,1)S(1)} collective-permute-done((bf16[256,256]{0,1:T(8,128)(2,1)S(1)}, bf16[256,256]{0,1:T(8,128)(2,1)S(1)}, u32[]{:S(2)}, u32[]{:S(2)}) %collective-permute-start) | collective-permute-done | bytes 131104 | tf_op jit(solution)/shard_map/while/body/eval_jaxpr/ppermute | solution.py:17
  371.7 11.1 %collective-permute-done = bf16[256,256]{0,1:T(8,128)(2,1)S(1)} collective-permute-done((bf16[256,256]{0,1:T(8,128)(2,1)S(1)}, bf16[256,256]{0,1:T(8,128)(2,1)S(1)}, u32[]{:S(2)}, u32[]{:S(2)}) %collective-permute-start) | collective-permute-done | bytes 131104 | tf_op jit(solution)/shard_map/while/body/eval_jaxpr/ppermute | solution.py:17
  384.7 1.9 collective-permute-start
  386.8 11.1 %collective-permute-done = bf16[256,256]{0,1:T(8,128)(2,1)S(1)} collective-permute-done((bf16[256,256]{0,1:T(8,128)(2,1)S(1)}, bf16[256,256]{0,1:T(8,128)(2,1)S(1)}, u32[]{:S(2)}, u32[]{:S(2)}) %collective-permute-start) | collective-permute-done | bytes 131104 | tf_op jit(solution)/shard_map/while/body/eval_jaxpr/ppermute | solution.py:17
  401.9 11.1 %collective-permute-done = bf16[256,256]{0,1:T(8,128)(2,1)S(1)} collective-permute-done((bf16[256,256]{0,1:T(8,128)(2,1)S(1)}, bf16[256,256]{0,1:T(8,128)(2,1)S(1)}, u32[]{:S(2)}, u32[]{:S(2)}) %collective-permute-start) | collective-permute-done | bytes 131104 | tf_op jit(solution)/shard_map/while/body/eval_jaxpr/ppermute | solution.py:17
  417.0 11.1 %collective-permute-done = bf16[256,256]{0,1:T(8,128)(2,1)S(1)} collective-permute-done((bf16[256,256]{0,1:T(8,128)(2,1)S(1)}, bf16[256,256]{0,1:T(8,128)(2,1)S(1)}, u32[]{:S(2)}, u32[]{:S(2)}) %collective-permute-start) | collective-permute-done | bytes 131104 | tf_op jit(solution)/shard_map/while/body/eval_jaxpr/ppermute | solution.py:17
  430.0 1.9 collective-permute-start
  432.1 11.1 %collective-permute-done = bf16[256,256]{0,1:T(8,128)(2,1)S(1)} collective-permute-done((bf16[256,256]{0,1:T(8,128)(2,1)S(1)}, bf16[256,256]{0,1:T(8,128)(2,1)S(1)}, u32[]{:S(2)}, u32[]{:S(2)}) %collective-permute-start) | collective-permute-done | bytes 131104 | tf_op jit(solution)/shard_map/while/body/eval_jaxpr/ppermute | solution.py:17
  447.1 11.1 %collective-permute-done = bf16[256,256]{0,1:T(8,128)(2,1)S(1)} collective-permute-done((bf16[256,256]{0,1:T(8,128)(2,1)S(1)}, bf16[256,256]{0,1:T(8,128)(2,1)S(1)}, u32[]{:S(2)}, u32[]{:S(2)}) %collective-permute-start) | collective-permute-done | bytes 131104 | tf_op jit(solution)/shard_map/while/body/eval_jaxpr/ppermute | solution.py:17
  462.2 11.1 %collective-permute-done = bf16[256,256]{0,1:T(8,128)(2,1)S(1)} collective-permute-done((bf16[256,256]{0,1:T(8,128)(2,1)S(1)}, bf16[256,256]{0,1:T(8,128)(2,1)S(1)}, u32[]{:S(2)}, u32[]{:S(2)}) %collective-permute-start) | collective-permute-done | bytes 131104 | tf_op jit(solution)/shard_map/while/body/eval_jaxpr/ppermute | solution.py:17
  475.3 1.9 collective-permute-start
  477.3 11.1 %collective-permute-done = bf16[256,256]{0,1:T(8,128)(2,1)S(1)} collective-permute-done((bf16[256,256]{0,1:T(8,128)(2,1)S(1)}, bf16[256,256]{0,1:T(8,128)(2,1)S(1)}, u32[]{:S(2)}, u32[]{:S(2)}) %collective-permute-start) | collective-permute-done | bytes 131104 | tf_op jit(solution)/shard_map/while/body/eval_jaxpr/ppermute | solution.py:17
  492.4 11.1 %collective-permute-done = bf16[256,256]{0,1:T(8,128)(2,1)S(1)} collective-permute-done((bf16[256,256]{0,1:T(8,128)(2,1)S(1)}, bf16[256,256]{0,1:T(8,128)(2,1)S(1)}, u32[]{:S(2)}, u32[]{:S(2)}) %collective-permute-start) | collective-permute-done | bytes 131104 | tf_op jit(solution)/shard_map/while/body/eval_jaxpr/ppermute | solution.py:17
  507.5 11.1 %collective-permute-done = bf16[256,256]{0,1:T(8,128)(2,1)S(1)} collective-permute-done((bf16[256,256]{0,1:T(8,128)(2,1)S(1)}, bf16[256,256]{0,1:T(8,128)(2,1)S(1)}, u32[]{:S(2)}, u32[]{:S(2)}) %collective-permute-start) | collective-permute-done | bytes 131104 | tf_op jit(solution)/shard_map/while/body/eval_jaxpr/ppermute | solution.py:17
  520.5 1.9 collective-permute-start
  522.6 11.1 %collective-permute-done = bf16[256,256]{0,1:T(8,128)(2,1)S(1)} collective-permute-done((bf16[256,256]{0,1:T(8,128)(2,1)S(1)}, bf16[256,256]{0,1:T(8,128)(2,1)S(1)}, u32[]{:S(2)}, u32[]{:S(2)}) %collective-permute-start) | collective-permute-done | bytes 131104 | tf_op jit(solution)/shard_map/while/body/eval_jaxpr/ppermute | solution.py:17
  537.7 11.1 %collective-permute-done = bf16[256,256]{0,1:T(8,128)(2,1)S(1)} collective-permute-done((bf16[256,256]{0,1:T(8,128)(2,1)S(1)}, bf16[256,256]{0,1:T(8,128)(2,1)S(1)}, u32[]{:S(2)}, u32[]{:S(2)}) %collective-permute-start) | collective-permute-done | bytes 131104 | tf_op jit(solution)/shard_map/while/body/eval_jaxpr/ppermute | solution.py:17
  552.8 11.1 %collective-permute-done = bf16[256,256]{0,1:T(8,128)(2,1)S(1)} collective-permute-done((bf16[256,256]{0,1:T(8,128)(2,1)S(1)}, bf16[256,256]{0,1:T(8,128)(2,1)S(1)}, u32[]{:S(2)}, u32[]{:S(2)}) %collective-permute-start) | collective-permute-done | bytes 131104 | tf_op jit(solution)/shard_map/while/body/eval_jaxpr/ppermute | solution.py:17
  565.8 1.9 collective-permute-start
  567.9 11.1 %collective-permute-done = bf16[256,256]{0,1:T(8,128)(2,1)S(1)} collective-permute-done((bf16[256,256]{0,1:T(8,128)(2,1)S(1)}, bf16[256,256]{0,1:T(8,128)(2,1)S(1)}, u32[]{:S(2)}, u32[]{:S(2)}) %collective-permute-start) | collective-permute-done | bytes 131104 | tf_op jit(solution)/shard_map/while/body/eval_jaxpr/ppermute | solution.py:17
  583.0 11.1 %collective-permute-done = bf16[256,256]{0,1:T(8,128)(2,1)S(1)} collective-permute-done((bf16[256,256]{0,1:T(8,128)(2,1)S(1)}, bf16[256,256]{0,1:T(8,128)(2,1)S(1)}, u32[]{:S(2)}, u32[]{:S(2)}) %collective-permute-start) | collective-permute-done | bytes 131104 | tf_op jit(solution)/shard_map/while/body/eval_jaxpr/ppermute | solution.py:17
  598.1 11.1 %collective-permute-done = bf16[256,256]{0,1:T(8,128)(2,1)S(1)} collective-permute-done((bf16[256,256]{0,1:T(8,128)(2,1)S(1)}, bf16[256,256]{0,1:T(8,128)(2,1)S(1)}, u32[]{:S(2)}, u32[]{:S(2)}) %collective-permute-start) | collective-permute-done | bytes 131104 | tf_op jit(solution)/shard_map/while/body/eval_jaxpr/ppermute | solution.py:17
  613.1 11.1 %collective-permute-done = bf16[256,256]{0,1:T(8,128)(2,1)S(1)} collective-permute-done((bf16[256,256]{0,1:T(8,128)(2,1)S(1)}, bf16[256,256]{0,1:T(8,128)(2,1)S(1)}, u32[]{:S(2)}, u32[]{:S(2)}) %collective-permute-start) | collective-permute-done | bytes 131104 | tf_op jit(solution)/shard_map/while/body/eval_jaxpr/ppermute | solution.py:17
  628.2 11.1 %collective-permute-done = bf16[256,256]{0,1:T(8,128)(2,1)S(1)} collective-permute-done((bf16[256,256]{0,1:T(8,128)(2,1)S(1)}, bf16[256,256]{0,1:T(8,128)(2,1)S(1)}, u32[]{:S(2)}, u32[]{:S(2)}) %collective-permute-start) | collective-permute-done | bytes 131104 | tf_op jit(solution)/shard_map/while/body/eval_jaxpr/ppermute | solution.py:17
  643.3 11.1 %collective-permute-done = bf16[256,256]{0,1:T(8,128)(2,1)S(1)} collective-permute-done((bf16[256,256]{0,1:T(8,128)(2,1)S(1)}, bf16[256,256]{0,1:T(8,128)(2,1)S(1)}, u32[]{:S(2)}, u32[]{:S(2)}) %collective-permute-start) | collective-permute-done | bytes 131104 | tf_op jit(solution)/shard_map/while/body/eval_jaxpr/ppermute | solution.py:17
  658.4 11.1 %collective-permute-done = bf16[256,256]{0,1:T(8,128)(2,1)S(1)} collective-permute-done((bf16[256,256]{0,1:T(8,128)(2,1)S(1)}, bf16[256,256]{0,1:T(8,128)(2,1)S(1)}, u32[]{:S(2)}, u32[]{:S(2)}) %collective-permute-start) | collective-permute-done | bytes 131104 | tf_op jit(solution)/shard_map/while/body/eval_jaxpr/ppermute | solution.py:17
  673.5 11.1 %collective-permute-done = bf16[256,256]{0,1:T(8,128)(2,1)S(1)} collective-permute-done((bf16[256,256]{0,1:T(8,128)(2,1)S(1)}, bf16[256,256]{0,1:T(8,128)(2,1)S(1)}, u32[]{:S(2)}, u32[]{:S(2)}) %collective-permute-start) | collective-permute-done | bytes 131104 | tf_op jit(solution)/shard_map/while/body/eval_jaxpr/ppermute | solution.py:17
  (356 shorter events, 116.4 us)
Async XLA Ops:
  7.2 91.5 %all-gather.3.cloned.1.call-start = ((), (), s32[]{:S(2)}) async-start(), calls=%async_computation.1 | async-start | bytes 5242880 | tf_op jit(solution)/shard_map/all_gather | solution.py:59
  7.9 5.0 copy-start.1
  7.9 23.6 %copy-start = (bf16[256,1024]{1,0:T(8,128)(2,1)S(1)}, bf16[256,1024]{1,0:T(8,128)(2,1)}, u32[]{:S(2)}) copy-start(bf16[256,1024]{1,0:T(8,128)(2,1)} %param.11) | copy-start | bytes 1572868
  12.1 19.8 %copy-start.2 = (s32[64,1]{0,1:T(1,128)S(1)}, s32[64,1]{0,1:T(1,128)}, u32[]{:S(2)}) copy-start(s32[64,1]{0,1:T(1,128)} %param.13) | copy-start | bytes 772
  12.2 181.1 %all-gather.5.cloned.1.call-start = ((), (), s32[]{:S(2)}) async-start(), calls=%async_computation.2 | async-start | bytes 4259840 | tf_op jit(solution)/shard_map/all_gather | solution.py:62
  202.4 485.8 %all-to-all-start = ((bf16[64,2,4,256]{3,2,1,0:T(4,128)(2,1)}), bf16[64,2,4,256]{3,2,1,0:T(4,128)(2,1)S(1)}, u32[]{:S(2)}, u32[]{:S(2)}) async-start(bf16[64,2,4,256]{3,2,1,0:T(4,128)(2,1)} %reshape.423), calls=%async_computation | async-start | bytes 524288 | tf_op jit(solution)/shard_map/all_to_all | solution.py:132
  209.8 9.2 %collective-permute-start = (bf16[256,256]{0,1:T(8,128)(2,1)S(1)}, bf16[256,256]{0,1:T(8,128)(2,1)S(1)}, u32[]{:S(2)}, u32[]{:S(2)}) collective-permute-start(bf16[256,256]{0,1:T(8,128)(2,1)S(1)} %get-tuple-element.308), channel_id=1, source_target_pairs={{0,4},{4,8},{8,12},{12,16},{16,20},{20,24},{24,28},{28,32},{32,36}... | collective-permute-start | bytes 393224 | tf_op jit(solution)/shard_map/while/body/eval_jaxpr/ppermute | solution.py:17
  220.9 10.2 %collective-permute-start = (bf16[256,256]{0,1:T(8,128)(2,1)S(1)}, bf16[256,256]{0,1:T(8,128)(2,1)S(1)}, u32[]{:S(2)}, u32[]{:S(2)}) collective-permute-start(bf16[256,256]{0,1:T(8,128)(2,1)S(1)} %get-tuple-element.308), channel_id=1, source_target_pairs={{0,4},{4,8},{8,12},{12,16},{16,20},{20,24},{24,28},{28,32},{32,36}... | collective-permute-start | bytes 393224 | tf_op jit(solution)/shard_map/while/body/eval_jaxpr/ppermute | solution.py:17
  233.0 13.8 %collective-permute-start = (bf16[256,256]{0,1:T(8,128)(2,1)S(1)}, bf16[256,256]{0,1:T(8,128)(2,1)S(1)}, u32[]{:S(2)}, u32[]{:S(2)}) collective-permute-start(bf16[256,256]{0,1:T(8,128)(2,1)S(1)} %get-tuple-element.308), channel_id=1, source_target_pairs={{0,4},{4,8},{8,12},{12,16},{16,20},{20,24},{24,28},{28,32},{32,36}... | collective-permute-start | bytes 393224 | tf_op jit(solution)/shard_map/while/body/eval_jaxpr/ppermute | solution.py:17
  248.7 13.3 %collective-permute-start = (bf16[256,256]{0,1:T(8,128)(2,1)S(1)}, bf16[256,256]{0,1:T(8,128)(2,1)S(1)}, u32[]{:S(2)}, u32[]{:S(2)}) collective-permute-start(bf16[256,256]{0,1:T(8,128)(2,1)S(1)} %get-tuple-element.308), channel_id=1, source_target_pairs={{0,4},{4,8},{8,12},{12,16},{16,20},{20,24},{24,28},{28,32},{32,36}... | collective-permute-start | bytes 393224 | tf_op jit(solution)/shard_map/while/body/eval_jaxpr/ppermute | solution.py:17
  263.9 13.3 %collective-permute-start = (bf16[256,256]{0,1:T(8,128)(2,1)S(1)}, bf16[256,256]{0,1:T(8,128)(2,1)S(1)}, u32[]{:S(2)}, u32[]{:S(2)}) collective-permute-start(bf16[256,256]{0,1:T(8,128)(2,1)S(1)} %get-tuple-element.308), channel_id=1, source_target_pairs={{0,4},{4,8},{8,12},{12,16},{16,20},{20,24},{24,28},{28,32},{32,36}... | collective-permute-start | bytes 393224 | tf_op jit(solution)/shard_map/while/body/eval_jaxpr/ppermute | solution.py:17
  279.1 13.2 %collective-permute-start = (bf16[256,256]{0,1:T(8,128)(2,1)S(1)}, bf16[256,256]{0,1:T(8,128)(2,1)S(1)}, u32[]{:S(2)}, u32[]{:S(2)}) collective-permute-start(bf16[256,256]{0,1:T(8,128)(2,1)S(1)} %get-tuple-element.308), channel_id=1, source_target_pairs={{0,4},{4,8},{8,12},{12,16},{16,20},{20,24},{24,28},{28,32},{32,36}... | collective-permute-start | bytes 393224 | tf_op jit(solution)/shard_map/while/body/eval_jaxpr/ppermute | solution.py:17
  294.2 13.2 %collective-permute-start = (bf16[256,256]{0,1:T(8,128)(2,1)S(1)}, bf16[256,256]{0,1:T(8,128)(2,1)S(1)}, u32[]{:S(2)}, u32[]{:S(2)}) collective-permute-start(bf16[256,256]{0,1:T(8,128)(2,1)S(1)} %get-tuple-element.308), channel_id=1, source_target_pairs={{0,4},{4,8},{8,12},{12,16},{16,20},{20,24},{24,28},{28,32},{32,36}... | collective-permute-start | bytes 393224 | tf_op jit(solution)/shard_map/while/body/eval_jaxpr/ppermute | solution.py:17
  309.3 13.2 %collective-permute-start = (bf16[256,256]{0,1:T(8,128)(2,1)S(1)}, bf16[256,256]{0,1:T(8,128)(2,1)S(1)}, u32[]{:S(2)}, u32[]{:S(2)}) collective-permute-start(bf16[256,256]{0,1:T(8,128)(2,1)S(1)} %get-tuple-element.308), channel_id=1, source_target_pairs={{0,4},{4,8},{8,12},{12,16},{16,20},{20,24},{24,28},{28,32},{32,36}... | collective-permute-start | bytes 393224 | tf_op jit(solution)/shard_map/while/body/eval_jaxpr/ppermute | solution.py:17
  324.3 13.2 %collective-permute-start = (bf16[256,256]{0,1:T(8,128)(2,1)S(1)}, bf16[256,256]{0,1:T(8,128)(2,1)S(1)}, u32[]{:S(2)}, u32[]{:S(2)}) collective-permute-start(bf16[256,256]{0,1:T(8,128)(2,1)S(1)} %get-tuple-element.308), channel_id=1, source_target_pairs={{0,4},{4,8},{8,12},{12,16},{16,20},{20,24},{24,28},{28,32},{32,36}... | collective-permute-start | bytes 393224 | tf_op jit(solution)/shard_map/while/body/eval_jaxpr/ppermute | solution.py:17
  339.4 13.2 %collective-permute-start = (bf16[256,256]{0,1:T(8,128)(2,1)S(1)}, bf16[256,256]{0,1:T(8,128)(2,1)S(1)}, u32[]{:S(2)}, u32[]{:S(2)}) collective-permute-start(bf16[256,256]{0,1:T(8,128)(2,1)S(1)} %get-tuple-element.308), channel_id=1, source_target_pairs={{0,4},{4,8},{8,12},{12,16},{16,20},{20,24},{24,28},{28,32},{32,36}... | collective-permute-start | bytes 393224 | tf_op jit(solution)/shard_map/while/body/eval_jaxpr/ppermute | solution.py:17
  354.5 13.2 %collective-permute-start = (bf16[256,256]{0,1:T(8,128)(2,1)S(1)}, bf16[256,256]{0,1:T(8,128)(2,1)S(1)}, u32[]{:S(2)}, u32[]{:S(2)}) collective-permute-start(bf16[256,256]{0,1:T(8,128)(2,1)S(1)} %get-tuple-element.308), channel_id=1, source_target_pairs={{0,4},{4,8},{8,12},{12,16},{16,20},{20,24},{24,28},{28,32},{32,36}... | collective-permute-start | bytes 393224 | tf_op jit(solution)/shard_map/while/body/eval_jaxpr/ppermute | solution.py:17
  369.6 13.2 %collective-permute-start = (bf16[256,256]{0,1:T(8,128)(2,1)S(1)}, bf16[256,256]{0,1:T(8,128)(2,1)S(1)}, u32[]{:S(2)}, u32[]{:S(2)}) collective-permute-start(bf16[256,256]{0,1:T(8,128)(2,1)S(1)} %get-tuple-element.308), channel_id=1, source_target_pairs={{0,4},{4,8},{8,12},{12,16},{16,20},{20,24},{24,28},{28,32},{32,36}... | collective-permute-start | bytes 393224 | tf_op jit(solution)/shard_map/while/body/eval_jaxpr/ppermute | solution.py:17
  384.7 13.2 %collective-permute-start = (bf16[256,256]{0,1:T(8,128)(2,1)S(1)}, bf16[256,256]{0,1:T(8,128)(2,1)S(1)}, u32[]{:S(2)}, u32[]{:S(2)}) collective-permute-start(bf16[256,256]{0,1:T(8,128)(2,1)S(1)} %get-tuple-element.308), channel_id=1, source_target_pairs={{0,4},{4,8},{8,12},{12,16},{16,20},{20,24},{24,28},{28,32},{32,36}... | collective-permute-start | bytes 393224 | tf_op jit(solution)/shard_map/while/body/eval_jaxpr/ppermute | solution.py:17
  399.8 13.2 %collective-permute-start = (bf16[256,256]{0,1:T(8,128)(2,1)S(1)}, bf16[256,256]{0,1:T(8,128)(2,1)S(1)}, u32[]{:S(2)}, u32[]{:S(2)}) collective-permute-start(bf16[256,256]{0,1:T(8,128)(2,1)S(1)} %get-tuple-element.308), channel_id=1, source_target_pairs={{0,4},{4,8},{8,12},{12,16},{16,20},{20,24},{24,28},{28,32},{32,36}... | collective-permute-start | bytes 393224 | tf_op jit(solution)/shard_map/while/body/eval_jaxpr/ppermute | solution.py:17
  414.9 13.2 %collective-permute-start = (bf16[256,256]{0,1:T(8,128)(2,1)S(1)}, bf16[256,256]{0,1:T(8,128)(2,1)S(1)}, u32[]{:S(2)}, u32[]{:S(2)}) collective-permute-start(bf16[256,256]{0,1:T(8,128)(2,1)S(1)} %get-tuple-element.308), channel_id=1, source_target_pairs={{0,4},{4,8},{8,12},{12,16},{16,20},{20,24},{24,28},{28,32},{32,36}... | collective-permute-start | bytes 393224 | tf_op jit(solution)/shard_map/while/body/eval_jaxpr/ppermute | solution.py:17
  430.0 13.2 %collective-permute-start = (bf16[256,256]{0,1:T(8,128)(2,1)S(1)}, bf16[256,256]{0,1:T(8,128)(2,1)S(1)}, u32[]{:S(2)}, u32[]{:S(2)}) collective-permute-start(bf16[256,256]{0,1:T(8,128)(2,1)S(1)} %get-tuple-element.308), channel_id=1, source_target_pairs={{0,4},{4,8},{8,12},{12,16},{16,20},{20,24},{24,28},{28,32},{32,36}... | collective-permute-start | bytes 393224 | tf_op jit(solution)/shard_map/while/body/eval_jaxpr/ppermute | solution.py:17
  445.1 13.2 %collective-permute-start = (bf16[256,256]{0,1:T(8,128)(2,1)S(1)}, bf16[256,256]{0,1:T(8,128)(2,1)S(1)}, u32[]{:S(2)}, u32[]{:S(2)}) collective-permute-start(bf16[256,256]{0,1:T(8,128)(2,1)S(1)} %get-tuple-element.308), channel_id=1, source_target_pairs={{0,4},{4,8},{8,12},{12,16},{16,20},{20,24},{24,28},{28,32},{32,36}... | collective-permute-start | bytes 393224 | tf_op jit(solution)/shard_map/while/body/eval_jaxpr/ppermute | solution.py:17
  460.2 13.2 %collective-permute-start = (bf16[256,256]{0,1:T(8,128)(2,1)S(1)}, bf16[256,256]{0,1:T(8,128)(2,1)S(1)}, u32[]{:S(2)}, u32[]{:S(2)}) collective-permute-start(bf16[256,256]{0,1:T(8,128)(2,1)S(1)} %get-tuple-element.308), channel_id=1, source_target_pairs={{0,4},{4,8},{8,12},{12,16},{16,20},{20,24},{24,28},{28,32},{32,36}... | collective-permute-start | bytes 393224 | tf_op jit(solution)/shard_map/while/body/eval_jaxpr/ppermute | solution.py:17
  475.3 13.2 %collective-permute-start = (bf16[256,256]{0,1:T(8,128)(2,1)S(1)}, bf16[256,256]{0,1:T(8,128)(2,1)S(1)}, u32[]{:S(2)}, u32[]{:S(2)}) collective-permute-start(bf16[256,256]{0,1:T(8,128)(2,1)S(1)} %get-tuple-element.308), channel_id=1, source_target_pairs={{0,4},{4,8},{8,12},{12,16},{16,20},{20,24},{24,28},{28,32},{32,36}... | collective-permute-start | bytes 393224 | tf_op jit(solution)/shard_map/while/body/eval_jaxpr/ppermute | solution.py:17
  490.3 13.2 %collective-permute-start = (bf16[256,256]{0,1:T(8,128)(2,1)S(1)}, bf16[256,256]{0,1:T(8,128)(2,1)S(1)}, u32[]{:S(2)}, u32[]{:S(2)}) collective-permute-start(bf16[256,256]{0,1:T(8,128)(2,1)S(1)} %get-tuple-element.308), channel_id=1, source_target_pairs={{0,4},{4,8},{8,12},{12,16},{16,20},{20,24},{24,28},{28,32},{32,36}... | collective-permute-start | bytes 393224 | tf_op jit(solution)/shard_map/while/body/eval_jaxpr/ppermute | solution.py:17
  505.4 13.2 %collective-permute-start = (bf16[256,256]{0,1:T(8,128)(2,1)S(1)}, bf16[256,256]{0,1:T(8,128)(2,1)S(1)}, u32[]{:S(2)}, u32[]{:S(2)}) collective-permute-start(bf16[256,256]{0,1:T(8,128)(2,1)S(1)} %get-tuple-element.308), channel_id=1, source_target_pairs={{0,4},{4,8},{8,12},{12,16},{16,20},{20,24},{24,28},{28,32},{32,36}... | collective-permute-start | bytes 393224 | tf_op jit(solution)/shard_map/while/body/eval_jaxpr/ppermute | solution.py:17
  520.5 13.2 %collective-permute-start = (bf16[256,256]{0,1:T(8,128)(2,1)S(1)}, bf16[256,256]{0,1:T(8,128)(2,1)S(1)}, u32[]{:S(2)}, u32[]{:S(2)}) collective-permute-start(bf16[256,256]{0,1:T(8,128)(2,1)S(1)} %get-tuple-element.308), channel_id=1, source_target_pairs={{0,4},{4,8},{8,12},{12,16},{16,20},{20,24},{24,28},{28,32},{32,36}... | collective-permute-start | bytes 393224 | tf_op jit(solution)/shard_map/while/body/eval_jaxpr/ppermute | solution.py:17
  535.6 13.2 %collective-permute-start = (bf16[256,256]{0,1:T(8,128)(2,1)S(1)}, bf16[256,256]{0,1:T(8,128)(2,1)S(1)}, u32[]{:S(2)}, u32[]{:S(2)}) collective-permute-start(bf16[256,256]{0,1:T(8,128)(2,1)S(1)} %get-tuple-element.308), channel_id=1, source_target_pairs={{0,4},{4,8},{8,12},{12,16},{16,20},{20,24},{24,28},{28,32},{32,36}... | collective-permute-start | bytes 393224 | tf_op jit(solution)/shard_map/while/body/eval_jaxpr/ppermute | solution.py:17
  550.7 13.2 %collective-permute-start = (bf16[256,256]{0,1:T(8,128)(2,1)S(1)}, bf16[256,256]{0,1:T(8,128)(2,1)S(1)}, u32[]{:S(2)}, u32[]{:S(2)}) collective-permute-start(bf16[256,256]{0,1:T(8,128)(2,1)S(1)} %get-tuple-element.308), channel_id=1, source_target_pairs={{0,4},{4,8},{8,12},{12,16},{16,20},{20,24},{24,28},{28,32},{32,36}... | collective-permute-start | bytes 393224 | tf_op jit(solution)/shard_map/while/body/eval_jaxpr/ppermute | solution.py:17
  565.8 13.2 %collective-permute-start = (bf16[256,256]{0,1:T(8,128)(2,1)S(1)}, bf16[256,256]{0,1:T(8,128)(2,1)S(1)}, u32[]{:S(2)}, u32[]{:S(2)}) collective-permute-start(bf16[256,256]{0,1:T(8,128)(2,1)S(1)} %get-tuple-element.308), channel_id=1, source_target_pairs={{0,4},{4,8},{8,12},{12,16},{16,20},{20,24},{24,28},{28,32},{32,36}... | collective-permute-start | bytes 393224 | tf_op jit(solution)/shard_map/while/body/eval_jaxpr/ppermute | solution.py:17
  580.9 13.2 %collective-permute-start = (bf16[256,256]{0,1:T(8,128)(2,1)S(1)}, bf16[256,256]{0,1:T(8,128)(2,1)S(1)}, u32[]{:S(2)}, u32[]{:S(2)}) collective-permute-start(bf16[256,256]{0,1:T(8,128)(2,1)S(1)} %get-tuple-element.308), channel_id=1, source_target_pairs={{0,4},{4,8},{8,12},{12,16},{16,20},{20,24},{24,28},{28,32},{32,36}... | collective-permute-start | bytes 393224 | tf_op jit(solution)/shard_map/while/body/eval_jaxpr/ppermute | solution.py:17
  596.0 13.2 %collective-permute-start = (bf16[256,256]{0,1:T(8,128)(2,1)S(1)}, bf16[256,256]{0,1:T(8,128)(2,1)S(1)}, u32[]{:S(2)}, u32[]{:S(2)}) collective-permute-start(bf16[256,256]{0,1:T(8,128)(2,1)S(1)} %get-tuple-element.308), channel_id=1, source_target_pairs={{0,4},{4,8},{8,12},{12,16},{16,20},{20,24},{24,28},{28,32},{32,36}... | collective-permute-start | bytes 393224 | tf_op jit(solution)/shard_map/while/body/eval_jaxpr/ppermute | solution.py:17
  611.1 13.2 %collective-permute-start = (bf16[256,256]{0,1:T(8,128)(2,1)S(1)}, bf16[256,256]{0,1:T(8,128)(2,1)S(1)}, u32[]{:S(2)}, u32[]{:S(2)}) collective-permute-start(bf16[256,256]{0,1:T(8,128)(2,1)S(1)} %get-tuple-element.308), channel_id=1, source_target_pairs={{0,4},{4,8},{8,12},{12,16},{16,20},{20,24},{24,28},{28,32},{32,36}... | collective-permute-start | bytes 393224 | tf_op jit(solution)/shard_map/while/body/eval_jaxpr/ppermute | solution.py:17
  626.2 13.2 %collective-permute-start = (bf16[256,256]{0,1:T(8,128)(2,1)S(1)}, bf16[256,256]{0,1:T(8,128)(2,1)S(1)}, u32[]{:S(2)}, u32[]{:S(2)}) collective-permute-start(bf16[256,256]{0,1:T(8,128)(2,1)S(1)} %get-tuple-element.308), channel_id=1, source_target_pairs={{0,4},{4,8},{8,12},{12,16},{16,20},{20,24},{24,28},{28,32},{32,36}... | collective-permute-start | bytes 393224 | tf_op jit(solution)/shard_map/while/body/eval_jaxpr/ppermute | solution.py:17
  641.2 13.2 %collective-permute-start = (bf16[256,256]{0,1:T(8,128)(2,1)S(1)}, bf16[256,256]{0,1:T(8,128)(2,1)S(1)}, u32[]{:S(2)}, u32[]{:S(2)}) collective-permute-start(bf16[256,256]{0,1:T(8,128)(2,1)S(1)} %get-tuple-element.308), channel_id=1, source_target_pairs={{0,4},{4,8},{8,12},{12,16},{16,20},{20,24},{24,28},{28,32},{32,36}... | collective-permute-start | bytes 393224 | tf_op jit(solution)/shard_map/while/body/eval_jaxpr/ppermute | solution.py:17
  656.3 13.2 %collective-permute-start = (bf16[256,256]{0,1:T(8,128)(2,1)S(1)}, bf16[256,256]{0,1:T(8,128)(2,1)S(1)}, u32[]{:S(2)}, u32[]{:S(2)}) collective-permute-start(bf16[256,256]{0,1:T(8,128)(2,1)S(1)} %get-tuple-element.308), channel_id=1, source_target_pairs={{0,4},{4,8},{8,12},{12,16},{16,20},{20,24},{24,28},{28,32},{32,36}... | collective-permute-start | bytes 393224 | tf_op jit(solution)/shard_map/while/body/eval_jaxpr/ppermute | solution.py:17
  671.4 13.2 %collective-permute-start = (bf16[256,256]{0,1:T(8,128)(2,1)S(1)}, bf16[256,256]{0,1:T(8,128)(2,1)S(1)}, u32[]{:S(2)}, u32[]{:S(2)}) collective-permute-start(bf16[256,256]{0,1:T(8,128)(2,1)S(1)} %get-tuple-element.308), channel_id=1, source_target_pairs={{0,4},{4,8},{8,12},{12,16},{16,20},{20,24},{24,28},{28,32},{32,36}... | collective-permute-start | bytes 393224 | tf_op jit(solution)/shard_map/while/body/eval_jaxpr/ppermute | solution.py:17
Sparse Core Ops, SparseCore 0:
  12.3 86.3 all-gather.2
  102.2 91.0 all-gather.4
where the time goes:
time: 707 us; the launch traced here: 696 us
  waiting for transfers between devices  491 us (69%)
  starting transfers between devices  89.8 us (13%)
  matrix products  54.4 us (8%)
  other arithmetic  20.8 us (3%)
  blocking collectives  18.4 us (3%)
  between operations  14.3 us (2%)
    ppermute x32, waiting for transfers between devices, shifted(): lax.ppermute(value, axis, [(source, source + steps) for source in range(i...  329 us
    all_gather x1, waiting for transfers between devices, on_device(): lax.all_gather(kv_weight, 'seq', axis=0, tiled=True)  94.5 us
    ppermute x32, starting transfers between devices, shifted(): lax.ppermute(value, axis, [(source, source + steps) for source in range(i...  82.3 us
    all_gather x1, waiting for transfers between devices, on_device(): gathered = lax.all_gather(normed, 'fs', axis=0, tiled=True)  66.3 us
    dot_general x33, matrix products, attend(): jnp.einsum('hgqk,khd->hgqd', rounded, values, preferred_element_type=jnp....  32.9 us
    pmin x1, blocking collectives, on_device(): starts = lax.pmin(firsts, 'seq')  18.4 us
    dot_general x33, matrix products, attend(): jnp.einsum('qhgd,khd->hgqk', query_heads, keys, preferred_element_type=jn...  16.1 us
  transfers between devices with their start and end apart: 35, of which 34 were waited for; matrix products, arithmetic and copies ran while one was open for 9% of the time, Pallas kernels for 0%

commit v1 on v0

v1 whole, which is shorter than its diff:
```python
import functools

import jax
import jax.numpy as jnp
from jax import lax
from jax.experimental import pallas as pl
from jax.experimental.pallas import tpu as pltpu
from jax.sharding import PartitionSpec as P

HD = 128
SEGS = 4
EPSILON = 1e-05
NEGATIVE = -1e30
LOG2E = 1.4426950408889634
MESH = pl.DeviceIdType.MESH
BLK = 256


def rotate_keys(keys, positions):
    half = keys.shape[-1] // 2
    freq = 10000.0 ** (-jnp.arange(half, dtype=jnp.float32) * 2.0 / keys.shape[-1])
    angle = positions.astype(jnp.float32)[:, None] * freq[None, :]
    cosine = jnp.cos(angle)[:, None, :]
    sine = jnp.sin(angle)[:, None, :]
    first = keys[..., :half]
    second = keys[..., half:]
    return jnp.concatenate(
        [first * cosine - second * sine, second * cosine + first * sine], axis=-1
    )


def pair_keys(projected, positions, head_size):
    rows = projected.shape[0]
    pairs = projected.reshape(rows, -1, 2, head_size)
    turned = rotate_keys(pairs[:, :, 0], positions)
    return jnp.stack([turned, pairs[:, :, 1]], axis=2).reshape(rows, -1).astype(jnp.bfloat16)


class Place:
    def __init__(self):
        s = lax.axis_index("seq")
        self.s = s
        self.f = lax.axis_index("fs")
        self.c = lax.rem(s, 2)
        self.z = lax.rem(lax.div(s, 2), 2)
        self.x = lax.rem(lax.div(s, 4), 4)
        self.y = lax.div(s, 16)

    def at(self, dy=0, dx=0, other_z=False, other_core=False):
        y = lax.rem(self.y + dy, 4)
        x = lax.rem(self.x + dx, 4)
        z = 1 - self.z if other_z else self.z
        c = 1 - self.c if other_core else self.c
        return (((y * 4 + x) * 2 + z) * 2 + c, self.f)


def remote(src, dst, send, recv, target):
    return pltpu.make_async_remote_copy(
        src_ref=src, dst_ref=dst, send_sem=send, recv_sem=recv, device_id=target, device_id_type=MESH
    )


def attend_kernel(
    kv_ref, q_ref, qseg_ref, bounds_ref, out_ref, buf, qa, kaug, m_ref, l_ref, acc_ref, ss, rs
):
    me = Place()
    c, z, x = me.c, me.z, me.x
    heads = q_ref.shape[1] // HD
    scale2 = (HD ** (-0.5)) * LOG2E

    core = me.at(other_core=True)
    opposite = me.at(other_z=True)
    partners = [core, opposite] + [me.at(dy=k) for k in (1, 2, 3)] + [me.at(dx=k) for k in (1, 2, 3)]
    barrier = pltpu.get_barrier_semaphore()
    for partner in partners:
        pl.semaphore_signal(barrier, inc=1, device_id=partner, device_id_type=MESH)
    buf[0, 0, z, c] = kv_ref[...]
    pl.semaphore_wait(barrier, len(partners))

    started = []

    def send(index, src, dst, target):
        copy = remote(src, dst, ss.at[index], rs.at[index], target)
        copy.start()
        started.append(copy)

    def arrived(index, dst):
        remote(dst, dst, ss.at[index], rs.at[index], core).wait_recv()

    send(0, kv_ref, buf.at[0, 0, z, c], core)
    send(1, kv_ref, buf.at[0, 0, z, c], opposite)

    for h in range(heads):
        qa[h, :, 0:HD] = q_ref[:, h * HD : (h + 1) * HD]
        qa[h, :, HD : 2 * HD] = qseg_ref[...]
        m_ref[h] = jnp.full((BLK, HD), NEGATIVE, jnp.float32)
        l_ref[h] = jnp.zeros((BLK, HD), jnp.float32)
        acc_ref[h] = jnp.zeros((BLK, HD), jnp.float32)

    low = bounds_ref[0:1, :]
    high = bounds_ref[1:2, :]
    quad_first = (me.y * 4 + x) * 4 * BLK
    token = me.s * BLK + lax.broadcasted_iota(jnp.int32, (BLK, 1), 0)

    def fold(blocks, first_key, causal):
        count = len(blocks) * BLK
        for i, block in enumerate(blocks):
            rows = pl.ds(i * BLK, BLK)
            kaug[rows, 0:HD] = block[:, 0:HD]
            key = first_key + i * BLK + lax.broadcasted_iota(jnp.int32, (BLK, HD), 0)
            inside = (key >= low) & (key < high)
            kaug[rows, HD : 2 * HD] = jnp.where(inside, 0.0, NEGATIVE).astype(jnp.bfloat16)
        values = jnp.concatenate([block[:, HD : 2 * HD] for block in blocks], axis=0)
        key_row = first_key + lax.broadcasted_iota(jnp.int32, (1, count), 1)

        def one_head(h, carry):
            scores = lax.dot_general(
                qa[h],
                kaug[0:count, :],
                (((1,), (1,)), ((), ())),
                preferred_element_type=jnp.float32,
            )
            if causal:
                scores = jnp.where(key_row <= token, scores, NEGATIVE)
            old = m_ref[h]
            new = jnp.maximum(old, jnp.max(scores, axis=1, keepdims=True))
            weights = jnp.exp2(scores * scale2 - new[:, 0:1] * scale2)
            factor = jnp.exp2((old - new) * scale2)
            m_ref[h] = new
            l_ref[h] = l_ref[h] * factor + jnp.sum(weights, axis=1, keepdims=True)
            update = jnp.dot(
                weights.astype(jnp.bfloat16), values, preferred_element_type=jnp.float32
            )
            acc_ref[h] = acc_ref[h] * factor + update
            return carry

        lax.fori_loop(0, heads, one_head, 0, unroll=2)

    def quad(rx, k):
        return [buf.at[rx, k, zz, cc] for zz in range(2) for cc in range(2)]

    arrived(0, buf.at[0, 0, z, 1 - c])
    fold([buf.at[0, 0, z, 0], buf.at[0, 0, z, 1]], quad_first + z * 2 * BLK, True)

    arrived(1, buf.at[0, 0, 1 - z, c])
    mine = lambda rx, k: buf.at[rx, k, :, c]
    send(2, buf.at[0, 0, 1 - z, c], buf.at[0, 0, 1 - z, c], core)
    send(3, mine(0, 0), mine(0, 1), me.at(dy=1))
    send(4, mine(0, 0), mine(0, 2), me.at(dy=2))
    arrived(2, buf.at[0, 0, 1 - z, 1 - c])
    fold([buf.at[0, 0, 1 - z, 0], buf.at[0, 0, 1 - z, 1]], quad_first + (1 - z) * 2 * BLK, True)

    order = (1, 3, 2)
    other = lambda rx, k: buf.at[rx, k, :, 1 - c]
    out_wrap = {rx: lax.div(x + rx, 4) for rx in order}
    in_wrap = {rx: jnp.where(x < rx, 1, 0) for rx in order}

    arrived(3, mine(0, 1))
    send(5, mine(0, 1), mine(0, 1), core)
    for rx in order:
        send(6 + rx, mine(0, 1), mine(rx, 1 - out_wrap[rx]), me.at(dx=rx))
    arrived(4, mine(0, 2))
    send(6, mine(0, 2), mine(0, 2), core)
    for rx in order:
        send(9 + rx, mine(0, 2 * out_wrap[rx]), mine(rx, out_wrap[rx]), me.at(dx=rx))
    arrived(5, other(0, 1))
    fold(quad(0, 1), quad_first - 16 * BLK, False)
    arrived(6, other(0, 2))
    fold(quad(0, 2), quad_first - 32 * BLK, False)

    stages = [(6 + rx, 12 + rx, rx, 1 - in_wrap[rx]) for rx in order]
    stages += [(9 + rx, 15 + rx, rx, in_wrap[rx]) for rx in order]

    def forward(stage):
        first, second, rx, k = stage
        arrived(first, mine(rx, k))
        send(second, mine(rx, k), mine(rx, k), core)

    forward(stages[0])
    for i, (first, second, rx, k) in enumerate(stages):
        if i + 1 < len(stages):
            forward(stages[i + 1])
        arrived(second, other(rx, k))
        fold(quad(rx, k), quad_first - (rx + 4 * k) * 4 * BLK, False)

    for h in range(heads):
        out_ref[:, h * HD : (h + 1) * HD] = (acc_ref[h] / l_ref[h]).astype(out_ref.dtype)
    for copy in started:
        copy.wait_send()


def attend(kv_block, queries, query_onehot, bounds):
    heads = queries.shape[1] // HD
    vmem = pl.BlockSpec(memory_space=pltpu.VMEM)
    return pl.pallas_call(
        attend_kernel,
        out_shape=jax.ShapeDtypeStruct(queries.shape, jnp.bfloat16),
        in_specs=[vmem] * 4,
        out_specs=vmem,
        scratch_shapes=[
            pltpu.VMEM((4, 3, 2, 2, BLK, 2 * HD), jnp.bfloat16),
            pltpu.VMEM((heads, BLK, 2 * HD), jnp.bfloat16),
            pltpu.VMEM((4 * BLK, 2 * HD), jnp.bfloat16),
            pltpu.VMEM((heads, BLK, HD), jnp.float32),
            pltpu.VMEM((heads, BLK, HD), jnp.float32),
            pltpu.VMEM((heads, BLK, HD), jnp.float32),
            pltpu.SemaphoreType.DMA((19,)),
            pltpu.SemaphoreType.DMA((19,)),
        ],
        compiler_params=pltpu.CompilerParams(
            collective_id=0, has_side_effects=True, vmem_limit_bytes=48 << 20
        ),
        cost_estimate=pl.CostEstimate(
            flops=9_000_000_000, bytes_accessed=2_000_000, transcendentals=17_000_000
        ),
    )(kv_block, queries, query_onehot, bounds)


def on_device(hidden, norm_gain, kv_weight, queries, segment_ids, page_owner):
    seq_count = lax.axis_size("seq")
    seq_place = lax.axis_index("seq")
    block_rows = segment_ids.shape[0]
    stream_rows = block_rows * seq_count
    anchor = seq_place * block_rows
    token_index = anchor + jnp.arange(block_rows, dtype=jnp.int32)
    labels = jnp.arange(SEGS, dtype=jnp.int32)
    member = segment_ids[:, None] == labels[None, :]
    firsts = jnp.min(jnp.where(member, token_index[:, None], stream_rows), axis=0)
    starts = lax.pmin(firsts, "seq")
    query_start = jnp.sum(jnp.where(member, starts[None, :], 0), axis=1)
    positions = token_index - query_start
    wide = hidden.astype(jnp.float32)
    stat = jnp.mean(wide * wide, axis=1, keepdims=True)
    normed = (wide * lax.rsqrt(stat + EPSILON) * norm_gain.astype(jnp.float32)[None, :]).astype(
        jnp.bfloat16
    )
    gathered = lax.all_gather(normed, "fs", axis=0, tiled=True)
    projected = jnp.dot(
        gathered,
        lax.all_gather(kv_weight, "seq", axis=0, tiled=True),
        preferred_element_type=jnp.float32,
    )
    kv_block = pair_keys(projected, positions, HD)

    lanes = jnp.arange(HD, dtype=jnp.int32)
    query_onehot = (segment_ids[:, None] == lanes[None, :]).astype(jnp.bfloat16)
    low = jnp.full((HD,), stream_rows, jnp.int32).at[:SEGS].set(starts)
    high = jnp.full((HD,), stream_rows, jnp.int32).at[: SEGS - 1].set(starts[1:])
    bounds = jnp.zeros((8, HD), jnp.int32).at[0].set(low).at[1].set(high)
    attended = attend(kv_block, queries, query_onehot, bounds)

    pages_block = page_owner.shape[0]
    page_rows = block_rows // pages_block
    capacity = max(2, 2 * pages_block // seq_count)
    owners = page_owner[:, 0]
    order = jnp.arange(pages_block, dtype=jnp.int32)
    earlier = (owners[None, :] == owners[:, None]) & (order[None, :] < order[:, None])
    rank = jnp.sum(earlier.astype(jnp.int32), axis=1)
    target = owners * capacity + rank
    select = (jnp.arange(seq_count * capacity, dtype=jnp.int32)[:, None] == target[None, :]).astype(
        jnp.bfloat16
    )
    columns_dev = kv_block.shape[1]
    pages = kv_block.reshape(pages_block, page_rows * columns_dev)
    outgoing = jnp.dot(select, pages, preferred_element_type=jnp.float32).astype(jnp.bfloat16)
    outgoing = outgoing.reshape(seq_count, capacity, page_rows, columns_dev)
    arrived = lax.all_to_all(outgoing, "seq", split_axis=0, concat_axis=0, tiled=True)
    kv_cache = arrived.reshape(1, seq_count, capacity, page_rows, columns_dev)
    return (attended, kv_cache)


def solution(mesh):
    placed = (P(("seq", "fs"), None), P(), P("seq", "fs"), P("seq", "fs"), P("seq"), P("seq", None))
    return jax.shard_map(
        on_device,
        mesh=mesh,
        in_specs=placed,
        out_specs=(P("seq", "fs"), P("seq", None, None, None, "fs")),
        check_vma=False,
    )
```

time: 707 us -> 300 us (0.42)
  waiting for transfers between devices: 491 us -> 162 us
  starting transfers between devices: 89.8 us -> 7.56 us
  Pallas kernels: 0 us -> 77.1 us
  matrix products: 54.4 us -> 5.41 us
  other arithmetic: 20.8 us -> 6.31 us
    ppermute x32 -> x0, waiting for transfers between devices: 329 us -> none  [shifted(): lax.ppermute(value, axis, [(source, source + steps) for source in range(i...]
    ppermute x32 -> x0, starting transfers between devices: 82.3 us -> none  [shifted(): lax.ppermute(value, axis, [(source, source + steps) for source in range(i...]
    pallas_call x0 -> x1, Pallas kernels: none -> 77.1 us  [attend(): pl.pallas_call(attend_kernel, out_shape=jax.ShapeDtypeStruct(queries.shap...]
    dot_general x66 -> x0, matrix products: 49 us -> none  [the longest x33 32.9 us: attend(): jnp.einsum('hgqk,khd->hgqd', rounded, values, preferred_element_type=jnp....]
    reduce_sum x33 -> x0, other arithmetic: 9.71 us -> none  [attend(): totals = totals * factor + jnp.sum(weights, axis=-1)]
  transfers between devices with their start and end apart: 35 -> 3, of which waited for: 34 -> 2; matrix products, arithmetic and copies ran while one was open for 9% -> 0% of each run, Pallas kernels for 0% -> 26%
where the time goes in v1:
time: 300 us; the launch traced here: 294 us
  waiting for transfers between devices  162 us (54%)
  Pallas kernels  77.1 us (26%)
  blocking collectives  18.4 us (6%)
  between operations  14.2 us (5%)
  starting transfers between devices  7.56 us (3%)
  other arithmetic  6.31 us (2%)
  matrix products  5.41 us (2%)
    all_gather x1, waiting for transfers between devices, on_device(): lax.all_gather(kv_weight, 'seq', axis=0, tiled=True)  94.5 us
    pallas_call x1, Pallas kernels, attend(): pl.pallas_call(attend_kernel, out_shape=jax.ShapeDtypeStruct(queries.shap...  77.1 us
    all_gather x1, waiting for transfers between devices, on_device(): gathered = lax.all_gather(normed, 'fs', axis=0, tiled=True)  66.7 us
    pmin x1, blocking collectives, on_device(): starts = lax.pmin(firsts, 'seq')  18.4 us
    all_to_all x1, starting transfers between devices, on_device(): lax.all_to_all(outgoing, 'seq', split_axis=0, concat_axis=0, tiled=True)  7.48 us
  transfers between devices with their start and end apart: 3, of which 2 were waited for; matrix products, arithmetic and copies ran while one was open for 0% of the time, Pallas kernels for 26%

profile of v1, /device:TPU:49, one launch (start us, length us, event | category | flops | bytes accessed | tf_op | source)
XLA Modules:
  0.0 293.8 jit_solution(1785523493433053015)
XLA Ops:
  7.2 0.0 copy-start.1
  7.2 0.0 copy-start.2
  7.2 0.0 all-gather.3.cloned.1.call-start
  7.2 0.7 convert_element_type.34
  8.0 1.5 fusion
  9.5 2.6 fusion.2
  12.1 0.0 all-gather.3.cloned.1.call-update
  12.1 0.0 all-gather.5.cloned.1.call-start
  12.2 0.7 all-gather.5.cloned.1.call-update
  12.9 0.0 copy-done.1
  12.9 0.1 select_reduce_fusion.1
  13.0 18.4 %pmin.7 = s32[4]{0:T(128)S(1)} all-reduce(s32[4]{0:T(128)S(1)} %select_reduce_fusion.1), channel_id=1, replica_groups=mesh['seq'=64,'fs'=4] {'seq'}, use_global_device_ids=true, to_apply=%region_2.3 | all-reduce | flops 4 | bytes 32 | tf_op jit(solution)/shard_map/pmin | solution.py:229
  31.4 0.1 slice_bitcast_fusion
  31.6 0.0 copy-done.2
  31.6 0.2 convert_reduce_fusion
  31.8 0.1 select_reduce_fusion
  31.9 0.1 fusion.9.qseg_ref
  32.0 0.0 copy-start
  32.0 66.7 %all-gather.3.cloned.1.call-done = bf16[256,8192]{1,0:T(8,128)(2,1)} async-done(((bf16[64,8192]{1,0:T(8,128)(2,1)}), bf16[256,8192]{1,0:T(8,128)(2,1)}) %all-gather.3.cloned.1.call-update) | async-done | bytes 4194320 | tf_op jit(solution)/shard_map/all_gather | solution.py:237
  98.7 94.5 %all-gather.5.cloned.1.call-done = bf16[8192,256]{1,0:T(8,128)(2,1)} async-done(((bf16[128,256]{1,0:T(8,128)(2,1)}), bf16[8192,256]{1,0:T(8,128)(2,1)}) %all-gather.5.cloned.1.call-update) | async-done | bytes 4194320 | tf_op jit(solution)/shard_map/all_gather | solution.py:240
  193.2 5.2 %fusion.12 = f32[256,256]{0,1:T(8,128)S(1)} fusion(bf16[256,8192]{1,0:T(8,128)(2,1)} %all-gather.3.cloned.1.call-done, bf16[8192,256]{1,0:T(8,128)(2,1)} %all-gather.5.cloned.1.call-done), kind=kOutput, calls=%fused_computation.35 | convolution fusion | flops 1073741824 | bytes 8650752 | tf_op jit(solution)/shard_map/dot_general | solution.py:238
  198.5 0.1 copy.13
  198.6 0.1 copy.12
  198.7 0.6 fusion.7
  199.3 0.1 pad_maximum_fusion
  199.4 0.3 maximum_convert_fusion
  199.6 0.1 convert_element_type.41
  199.7 0.2 convolution_convert_fusion
  200.0 0.9 reshape.235
  200.8 7.5 %all-to-all-start = ((bf16[64,2,4,256]{3,2,1,0:T(4,128)(2,1)}), bf16[64,2,4,256]{3,2,1,0:T(4,128)(2,1)S(1)}, u32[]{:S(2)}, u32[]{:S(2)}) async-start(bf16[64,2,4,256]{3,2,1,0:T(4,128)(2,1)} %reshape.235), calls=%async_computation | async-start | bytes 524288 | tf_op jit(solution)/shard_map/all_to_all | solution.py:267
  208.3 0.0 copy-done
  208.3 77.1 %shard_map.77 = bf16[256,1024]{1,0:T(8,128)(2,1)S(1)} custom-call(bf16[256,256]{1,0:T(8,128)(2,1)S(1)} %bitcast.20, bf16[256,1024]{1,0:T(8,128)(2,1)S(1)} %copy-done, bf16[256,128]{1,0:T(8,128)(2,1)S(1)} %fusion.9.qseg_ref, s32[8,128]{1,0:T(8,128)S(1)} %scatter.19.bounds_ref), custom_call_target="tpu_custom_call" | custom-call | flops 8999999488 | bytes 2000000 | tf_op jit(solution)/shard_map/pallas_call | solution.py:195
  285.4 0.0 all-to-all-done
  285.4 0.8 copy.20
  286.2 0.7 copy.21
  (11 shorter events, 0.1 us)
Async XLA Ops:
  7.2 5.7 %copy-start.1 = (s32[256]{0:T(256)S(1)}, s32[256]{0:T(256)}, u32[]{:S(2)}) copy-start(s32[256]{0:T(256)} %param.18) | copy-start | bytes 3076
  7.2 24.4 %copy-start.2 = (s32[64,1]{0,1:T(1,128)S(1)}, s32[64,1]{0,1:T(1,128)}, u32[]{:S(2)}) copy-start(s32[64,1]{0,1:T(1,128)} %param.19) | copy-start | bytes 772
  7.2 91.5 %all-gather.3.cloned.1.call-start = ((), (), s32[]{:S(2)}) async-start(), calls=%async_computation.1 | async-start | bytes 5242880 | tf_op jit(solution)/shard_map/all_gather | solution.py:237
  12.1 181.1 %all-gather.5.cloned.1.call-start = ((), (), s32[]{:S(2)}) async-start(), calls=%async_computation.2 | async-start | bytes 4259840 | tf_op jit(solution)/shard_map/all_gather | solution.py:240
  32.0 176.4 %copy-start = (bf16[256,1024]{1,0:T(8,128)(2,1)S(1)}, bf16[256,1024]{1,0:T(8,128)(2,1)}, u32[]{:S(2)}) copy-start(bf16[256,1024]{1,0:T(8,128)(2,1)} %q_ref.1) | copy-start | bytes 1572868
  200.8 84.6 %all-to-all-start = ((bf16[64,2,4,256]{3,2,1,0:T(4,128)(2,1)}), bf16[64,2,4,256]{3,2,1,0:T(4,128)(2,1)S(1)}, u32[]{:S(2)}, u32[]{:S(2)}) async-start(bf16[64,2,4,256]{3,2,1,0:T(4,128)(2,1)} %reshape.235), calls=%async_computation | async-start | bytes 524288 | tf_op jit(solution)/shard_map/all_to_all | solution.py:267
Sparse Core Ops, SparseCore 0:
  12.3 86.3 all-gather.2
  102.1 91.0 all-gather.4

commit v2 on v1

--- a/solution.py
+++ b/solution.py
@@ -58,6 +58,229 @@
     return pltpu.make_async_remote_copy(
         src_ref=src, dst_ref=dst, send_sem=send, recv_sem=recv, device_id=target, device_id_type=MESH
     )
+
+
+def project_kernel(
+    hid_ref, gain_ref, w_ref, first_ref, out_ref, starts_ref, nb, wb, fb, acc, res, got, ss, rs
+):
+    me = Place()
+    c, z, x, y, f = me.c, me.z, me.x, me.y, me.f
+    parity, group = lax.rem(f, 2), lax.div(f, 2)
+    head = parity + 2 * c
+    twin = lax.rem(f + 2, 4)
+    mate = f + 1 - 2 * parity
+    home = c == group
+    chunks, rows, cols = nb.shape[2], nb.shape[3], nb.shape[4]
+
+    def near(zz, cc, ff):
+        return (((y * 4 + x) * 2 + zz) * 2 + cc, ff)
+
+    core = near(z, 1 - c, f)
+    ring_x = {k: me.at(dx=k) for k in (1, 2, 3)}
+    ring_y = {k: me.at(dy=k) for k in (1, 2, 3)}
+    cube = [near(zz, cc, ff) for ff in (f, twin) for zz in (z, 1 - z) for cc in (c, 1 - c)][1:]
+    partners = cube + [near(z, c, mate)] + list(ring_x.values()) + list(ring_y.values())
+    barrier = pltpu.get_barrier_semaphore()
+    for partner in partners:
+        pl.semaphore_signal(barrier, inc=1, device_id=partner, device_id_type=MESH)
+    pl.semaphore_wait(barrier, len(partners))
+
+    started = []
+
+    def send(index, src, dst, target, recv=None):
+        recv = index if recv is None else recv
+        copy = remote(src, dst, ss.at[index], rs.at[recv], target)
+        copy.start()
+        started.append(copy)
+
+    def arrived(index, dst):
+        remote(dst, dst, ss.at[index], rs.at[index], core).wait_recv()
+
+    quad = y * 4 + x
+    shard = 2 * z + c
+    rows_w = w_ref.shape[0]
+
+    def piece(zz, cc):
+        return wb.at[quad, zz, pl.ds(pl.multiple_of(cc * rows_w, rows_w), rows_w)]
+
+    def seed_to_core():
+        return remote(w_ref, piece(z, c), ss.at[0], rs.at[shard], core)
+
+    @pl.when(home)
+    def _():
+        wb[quad, z, pl.ds(pl.multiple_of(c * rows_w, rows_w), rows_w)] = w_ref[...]
+
+    @pl.when(jnp.logical_not(home))
+    def _():
+        seed_to_core().start()
+
+    send(1, w_ref, piece(z, c), near(z, group, twin), shard)
+    send(2, w_ref, piece(z, c), near(1 - z, group, f), shard)
+    send(3, w_ref, piece(z, c), near(1 - z, group, twin), shard)
+    send(4, first_ref, fb.at[0], core)
+    send(5, first_ref, fb.at[1], near(1 - z, c, f))
+    send(6, first_ref, fb.at[2], near(1 - z, 1 - c, f))
+
+    total = jnp.zeros((rows, 1), jnp.float32)
+    for i in range(chunks):
+        wide = hid_ref[:, i * cols : (i + 1) * cols].astype(jnp.float32)
+        total = total + jnp.sum(wide * wide, axis=1, keepdims=True)
+    factor = lax.rsqrt(total / (chunks * cols) + EPSILON)
+    for i in range(chunks):
+        wide = hid_ref[:, i * cols : (i + 1) * cols].astype(jnp.float32)
+        gain = gain_ref[:, i * cols : (i + 1) * cols].astype(jnp.float32)
+        nb[c, parity, i] = (wide * factor * gain).astype(jnp.bfloat16)
+        send(13 + i, nb.at[c, parity, i], nb.at[c, parity, i], near(z, c, mate))
+        send(17 + i, nb.at[c, parity, i], nb.at[c, parity, i], core)
+
+    def seed_arrived(zz):
+        for cc in (0, 1):
+            own = jnp.logical_and(home, shard == 2 * zz + cc)
+
+            @pl.when(jnp.logical_not(own))
+            def _():
+                arrived(2 * zz + cc, piece(zz, cc))
+
+    half = lambda yy, xx, hh: wb.at[yy * 4 + xx, hh]
+    back = lambda v, k: lax.rem(v + 4 - k, 4)
+    order = (1, 3, 2)
+    seed_arrived(0)
+    for k in order:
+        send(24 + k, half(y, x, 0), half(y, x, 0), ring_x[k])
+    seed_arrived(1)
+    for k in order:
+        send(27 + k, half(y, x, 1), half(y, x, 1), ring_y[k])
+
+    a2 = lambda k, j: 31 + (k - 1) * 4 + j
+    b2 = lambda k, j: 43 + (k - 1) * 4 + j
+
+    def spread(j):
+        ya, xa = y, back(x, j)
+        yb, xb = back(y, j), x
+        if j:
+            arrived(24 + j, half(ya, xa, 0))
+        for k in order:
+            send(a2(k, j), half(ya, xa, 0), half(ya, xa, 0), ring_y[k])
+        if j:
+            arrived(27 + j, half(yb, xb, 1))
+        for k in order:
+            send(b2(k, j), half(yb, xb, 1), half(yb, xb, 1), ring_x[k])
+
+    def forward(i):
+        arrived(13 + i, nb.at[c, 1 - parity, i])
+        send(21 + i, nb.at[c, 1 - parity, i], nb.at[c, 1 - parity, i], core)
+
+    spread(0)
+    for i in range(3):
+        arrived(4 + i, fb.at[i])
+    fb[3] = jnp.minimum(jnp.minimum(first_ref[...], fb[0]), jnp.minimum(fb[1], fb[2]))
+    for k in order:
+        send(6 + k, fb.at[3], fb.at[3 + k], ring_x[k])
+    forward(0)
+    spread(1)
+    spread(3)
+    forward(1)
+    spread(2)
+    for k in order:
+        arrived(6 + k, fb.at[3 + k])
+    fb[7] = jnp.minimum(jnp.minimum(fb[3], fb[4]), jnp.minimum(fb[5], fb[6]))
+    for k in order:
+        send(9 + k, fb.at[7], fb.at[7 + k], ring_y[k])
+    forward(2)
+    forward(3)
+    for k in order:
+        arrived(9 + k, fb.at[7 + k])
+    starts_ref[...] = jnp.minimum(jnp.minimum(fb[7], fb[8]), jnp.minimum(fb[9], fb[10]))
+    for i in range(chunks):
+        arrived(17 + i, nb.at[1 - c, parity, i])
+        arrived(21 + i, nb.at[1 - c, 1 - parity, i])
+
+    acc[...] = jnp.zeros_like(acc)
+
+    def multiply(yy, xx, hh):
+        columns = pl.ds(pl.multiple_of(xx * 512 + hh * 256, 256), 256)
+        lhs = nb[:, :, yy, :, columns].reshape(4 * rows, 256)
+        acc[...] += jnp.dot(lhs, wb[yy * 4 + xx, hh], preferred_element_type=jnp.float32)
+
+    multiply(y, x, 0)
+    multiply(y, x, 1)
+    for j in order:
+        multiply(y, back(x, j), 0)
+        multiply(back(y, j), x, 1)
+    for j in (0, 1, 3, 2):
+        for k in order:
+            yy, xx = back(y, k), back(x, j)
+            arrived(a2(k, j), half(yy, xx, 0))
+            multiply(yy, xx, 0)
+            yy, xx = back(y, j), back(x, k)
+            arrived(b2(k, j), half(yy, xx, 1))
+            multiply(yy, xx, 1)
+
+    res[...] = acc[...].reshape(res.shape)
+
+    def result_to(cc, ff, index):
+        return remote(res.at[cc], got.at[group], ss.at[index], rs.at[55 + group], near(z, cc, ff))
+
+    @pl.when(home)
+    def _():
+        result_to(1 - c, f, 55).start()
+        got[group] = res[c]
+
+    @pl.when(jnp.logical_not(home))
+    def _():
+        result_to(0, twin, 55).start()
+        result_to(1, twin, 56).start()
+
+    for g in (0, 1):
+
+        @pl.when(jnp.logical_not(jnp.logical_and(home, group == g)))
+        def _():
+            arrived(55 + g, got.at[g])
+
+    out_ref[...] = got[...].reshape(out_ref.shape)
+    for copy in started:
+        copy.wait_send()
+
+    @pl.when(home)
+    def _():
+        result_to(1 - c, f, 55).wait_send()
+
+    @pl.when(jnp.logical_not(home))
+    def _():
+        seed_to_core().wait_send()
+        result_to(0, twin, 55).wait_send()
+        result_to(1, twin, 56).wait_send()
+
+
+def project(hidden, gain, weight, firsts):
+    rows, width = hidden.shape
+    columns = weight.shape[1]
+    vmem = pl.BlockSpec(memory_space=pltpu.VMEM)
+    return pl.pallas_call(
+        project_kernel,
+        out_shape=(
+            jax.ShapeDtypeStruct((4 * rows, columns), jnp.float32),
+            jax.ShapeDtypeStruct((8, HD), jnp.int32),
+        ),
+        in_specs=[vmem] * 4,
+        out_specs=(vmem, vmem),
+        scratch_shapes=[
+            pltpu.VMEM((2, 2, 4, rows, width // 4), jnp.bfloat16),
+            pltpu.VMEM((16, 2, width // 32, columns), jnp.bfloat16),
+            pltpu.VMEM((11, 8, HD), jnp.int32),
+            pltpu.VMEM((4 * rows, columns), jnp.float32),
+            pltpu.VMEM((2, 2 * rows, columns), jnp.float32),
+            pltpu.VMEM((2, 2 * rows, columns), jnp.float32),
+            pltpu.SemaphoreType.DMA((57,)),
+            pltpu.SemaphoreType.DMA((57,)),
+        ],
+        compiler_params=pltpu.CompilerParams(
+            collective_id=1, has_side_effects=True, vmem_limit_bytes=48 << 20
+        ),
+        cost_estimate=pl.CostEstimate(
+            flops=1_100_000_000, bytes_accessed=2_000_000, transcendentals=0
+        ),
+    )(hidden, gain, weight, firsts)
 
 
 def attend_kernel(
@@ -226,20 +449,11 @@
     labels = jnp.arange(SEGS, dtype=jnp.int32)
     member = segment_ids[:, None] == labels[None, :]
     firsts = jnp.min(jnp.where(member, token_index[:, None], stream_rows), axis=0)
-    starts = lax.pmin(firsts, "seq")
+    first_tile = jnp.broadcast_to(jnp.pad(firsts, (0, HD - SEGS))[None, :], (8, HD))
+    projected, start_tile = project(hidden, norm_gain[None, :], kv_weight, first_tile)
+    starts = start_tile[0, :SEGS]
     query_start = jnp.sum(jnp.where(member, starts[None, :], 0), axis=1)
     positions = token_index - query_start
-    wide = hidden.astype(jnp.float32)
-    stat = jnp.mean(wide * wide, axis=1, keepdims=True)
-    normed = (wide * lax.rsqrt(stat + EPSILON) * norm_gain.astype(jnp.float32)[None, :]).astype(
-        jnp.bfloat16
-    )
-    gathered = lax.all_gather(normed, "fs", axis=0, tiled=True)
-    projected = jnp.dot(
-        gathered,
-        lax.all_gather(kv_weight, "seq", axis=0, tiled=True),
-        preferred_element_type=jnp.float32,
-    )
     kv_block = pair_keys(projected, positions, HD)
 
     lanes = jnp.arange(HD, dtype=jnp.int32)

time: 300 us -> 157 us (0.52)
  the two profiles are of different devices: /device:TPU:49 before, /device:TPU:1 now
where the time goes in v2:
time: 157 us
  Pallas kernels  139 us (89%)
  starting transfers between devices  7.89 us (5%)
  local copies, waits for them, and re-layouts  6.43 us (4%)
  other arithmetic  2.12 us (1%)
    pallas_call x1, Pallas kernels, attend(): pl.pallas_call(attend_kernel, out_shape=jax.ShapeDtypeStruct(queries.shap...  78.9 us
    pallas_call x1, Pallas kernels, project(): pl.pallas_call(project_kernel, out_shape=(jax.ShapeDtypeStruct((4 * rows,...  60.5 us
    all_to_all x1, starting transfers between devices, on_device(): lax.all_to_all(outgoing, 'seq', split_axis=0, concat_axis=0, tiled=True)  7.89 us
    unnamed x13, local copies, waits for them, and re-layouts  4.07 us
  transfers between devices with their start and end apart: 1, of which 0 were waited for; matrix products, arithmetic and copies ran while one was open for 0% of the time, Pallas kernels for 50%

profile of v2, /device:TPU:1, one launch (start us, length us, event | category | flops | bytes accessed | tf_op | source)
XLA Modules:
  0.0 156.9 jit_solution(2461179186438574831)
XLA Ops:
  0.6 0.0 copy-start.2
  0.7 0.7 broadcast_in_dim.30.gain_ref
  1.4 0.8 select_reduce_fusion.1
  2.2 0.0 copy-done.2
  2.2 0.0 copy-start
  2.3 1.2 copy-done
  3.5 60.5 %shard_map.77 = (f32[256,256]{1,0:T(8,128)S(1)}, s32[8,128]{1,0:T(8,128)S(1)}) custom-call(bf16[64,8192]{1,0:T(8,128)(2,1)S(1)} %copy-done, bf16[1,8192]{1,0:T(2,128)(2,1)S(1)} %broadcast_in_dim.30.gain_ref, bf16[128,256]{1,0:T(8,128)(2,1)S(1)} %copy-done.2, s32[8,128]{1,0:T(8,128)S(1)} %broadcast_in_dim.33.first_ref), custom_call_target="tpu_custom_call" | custom-call | flops 1100000000 | bytes 2000000 | tf_op jit(solution)/shard_map/pallas_call | solution.py:259
  64.0 0.1 reshape.220
  64.1 0.1 slice.77
  64.2 0.1 slice.80
  64.4 0.0 copy-start.3
  64.4 0.7 copy-done.3
  65.1 0.1 select_reduce_fusion
  65.2 0.6 fusion.4
  65.7 0.1 pad_maximum_fusion
  65.8 0.3 maximum_convert_fusion
  66.1 0.1 convert_element_type.29
  66.2 0.0 copy-start.4
  66.2 0.6 copy-done.4
  66.8 0.2 convert_reduce_fusion
  67.0 0.2 convolution_convert_fusion
  67.2 0.9 reshape.221
  68.1 0.0 copy-start.1
  68.1 7.9 %all-to-all-start = ((bf16[64,2,4,256]{3,2,1,0:T(4,128)(2,1)}), bf16[64,2,4,256]{3,2,1,0:T(4,128)(2,1)S(1)}, u32[]{:S(2)}, u32[]{:S(2)}) async-start(bf16[64,2,4,256]{3,2,1,0:T(4,128)(2,1)} %reshape.221), calls=%async_computation | async-start | bytes 524288 | tf_op jit(solution)/shard_map/all_to_all | solution.py:481
  76.0 0.1 slice.76
  76.1 0.1 fusion.6.qseg_ref
  76.3 0.2 scatter.19.bounds_ref
  76.5 0.0 copy-done.1
  76.5 78.9 %shard_map.78 = bf16[256,1024]{1,0:T(8,128)(2,1)S(1)} custom-call(bf16[256,256]{1,0:T(8,128)(2,1)S(1)} %bitcast.18, bf16[256,1024]{1,0:T(8,128)(2,1)S(1)} %copy-done.1, bf16[256,128]{1,0:T(8,128)(2,1)S(1)} %fusion.6.qseg_ref, s32[8,128]{1,0:T(8,128)S(1)} %scatter.19.bounds_ref), custom_call_target="tpu_custom_call" | custom-call | flops 8999999488 | bytes 2000000 | tf_op jit(solution)/shard_map/pallas_call | solution.py:418
  155.4 0.0 all-to-all-done
  155.4 0.8 copy.16
  156.2 0.7 copy.17
  (10 shorter events, 0.1 us)
Async XLA Ops:
  0.6 1.6 %copy-start.2 = (bf16[128,256]{1,0:T(8,128)(2,1)S(1)}, bf16[128,256]{1,0:T(8,128)(2,1)}, u32[]{:S(2)}) copy-start(bf16[128,256]{1,0:T(8,128)(2,1)} %w_ref.1) | copy-start | bytes 196612
  2.2 1.2 copy-start
  64.4 0.7 copy-start.3
  66.2 0.7 copy-start.4
  68.1 8.3 %copy-start.1 = (bf16[256,1024]{1,0:T(8,128)(2,1)S(1)}, bf16[256,1024]{1,0:T(8,128)(2,1)}, u32[]{:S(2)}) copy-start(bf16[256,1024]{1,0:T(8,128)(2,1)} %q_ref.1) | copy-start | bytes 1572868
  68.1 87.3 %all-to-all-start = ((bf16[64,2,4,256]{3,2,1,0:T(4,128)(2,1)}), bf16[64,2,4,256]{3,2,1,0:T(4,128)(2,1)S(1)}, u32[]{:S(2)}, u32[]{:S(2)}) async-start(bf16[64,2,4,256]{3,2,1,0:T(4,128)(2,1)} %reshape.221), calls=%async_computation | async-start | bytes 524288 | tf_op jit(solution)/shard_map/all_to_all | solution.py:481

commit v3 on v2

--- a/solution.py
+++ b/solution.py
@@ -36,6 +36,10 @@
     return jnp.stack([turned, pairs[:, :, 1]], axis=2).reshape(rows, -1).astype(jnp.bfloat16)
 
 
+def wrap(value, count):
+    return value - count * (value >= count).astype(jnp.int32)
+
+
 class Place:
     def __init__(self):
         s = lax.axis_index("seq")
@@ -47,8 +51,8 @@
         self.y = lax.div(s, 16)
 
     def at(self, dy=0, dx=0, other_z=False, other_core=False):
-        y = lax.rem(self.y + dy, 4)
-        x = lax.rem(self.x + dx, 4)
+        y = wrap(self.y + dy, 4)
+        x = wrap(self.x + dx, 4)
         z = 1 - self.z if other_z else self.z
         c = 1 - self.c if other_core else self.c
         return (((y * 4 + x) * 2 + z) * 2 + c, self.f)
@@ -284,151 +288,221 @@
 
 
 def attend_kernel(
-    kv_ref, q_ref, qseg_ref, bounds_ref, out_ref, buf, qa, kaug, m_ref, l_ref, acc_ref, ss, rs
+    kv_ref, q_ref, qseg_ref, bounds_ref, pages_ref, out_ref, cache_ref,
+    buf, pages, qa, m_ref, l_ref, acc_ref, ss, rs
 ):
     me = Place()
     c, z, x = me.c, me.z, me.x
     heads = q_ref.shape[1] // HD
+    owners = pages_ref.shape[0]
     scale2 = (HD ** (-0.5)) * LOG2E
-
     core = me.at(other_core=True)
     opposite = me.at(other_z=True)
-    partners = [core, opposite] + [me.at(dy=k) for k in (1, 2, 3)] + [me.at(dx=k) for k in (1, 2, 3)]
+
+    def peer(distance):
+        return (wrap(me.s + distance, owners), me.f)
+
     barrier = pltpu.get_barrier_semaphore()
-    for partner in partners:
-        pl.semaphore_signal(barrier, inc=1, device_id=partner, device_id_type=MESH)
+
+    def greet(distance, carry):
+        pl.semaphore_signal(barrier, inc=1, device_id=peer(distance), device_id_type=MESH)
+        return carry
+
+    lax.fori_loop(1, owners, greet, 0)
     buf[0, 0, z, c] = kv_ref[...]
-    pl.semaphore_wait(barrier, len(partners))
-
-    started = []
+    pages[me.s] = pages_ref[me.s]
+    pl.semaphore_wait(barrier, owners - 1)
 
     def send(index, src, dst, target):
-        copy = remote(src, dst, ss.at[index], rs.at[index], target)
-        copy.start()
-        started.append(copy)
+        remote(src, dst, ss.at[index], rs.at[index], target).start()
 
     def arrived(index, dst):
         remote(dst, dst, ss.at[index], rs.at[index], core).wait_recv()
 
-    send(0, kv_ref, buf.at[0, 0, z, c], core)
-    send(1, kv_ref, buf.at[0, 0, z, c], opposite)
+    def block(rx, k, zi, cc):
+        return buf.at[rx, k, wrap(z + zi, 2), cc]
+
+    def mine(rx, k, zi):
+        return block(rx, k, zi, c)
+
+    order = (1, 3, 2)
+    out_wrap = {rx: (x + rx >= 4).astype(jnp.int32) for rx in order}
+    in_wrap = {rx: (x < rx).astype(jnp.int32) for rx in order}
+    x1 = lambda rx, zi: 11 + 2 * (rx - 1) + zi
+    x2 = lambda rx, zi: 17 + 2 * (rx - 1) + zi
+
+    def second(rx, zi):
+        w = out_wrap[rx]
+        return remote(
+            mine(0, 2 * w, zi), mine(rx, w, zi), ss.at[x2(rx, zi)], rs.at[x2(rx, zi)], me.at(dx=rx)
+        )
+
+    def send_second(zi, wraps):
+        for rx in order:
+
+            @pl.when(out_wrap[rx] == wraps)
+            def _():
+                second(rx, zi).start()
+
+    def send_y(zi):
+        send(3 + zi, mine(0, 0, zi), mine(0, 1, zi), me.at(dy=1))
+        send(5 + zi, mine(0, 0, zi), mine(0, 2, zi), me.at(dy=2))
+        send_second(zi, 0)
+
+    def send_first(zi):
+        for rx in order:
+            send(x1(rx, zi), mine(0, 1, zi), mine(rx, 1 - out_wrap[rx], zi), me.at(dx=rx))
+
+    def forward(first, then, rx, k, zi):
+        arrived(first, mine(rx, k, zi))
+        send(then, mine(rx, k, zi), mine(rx, k, zi), core)
+
+    units = [
+        (0, 0, 0, None, 0),
+        (0, 1, 0, 3, 7),
+        (0, 2, 0, 5, 9),
+        (0, 0, 1, 1, 2),
+        (0, 1, 1, 4, 8),
+        (0, 2, 1, 6, 10),
+    ]
+    for zi in (0, 1):
+        units += [(rx, 1 - in_wrap[rx], zi, x1(rx, zi), x1(rx, zi) + 12) for rx in order]
+        units += [(rx, in_wrap[rx], zi, x2(rx, zi), x2(rx, zi) + 12) for rx in order]
+    turn = [0, 1, 2, 3, 6, 7, 8, 4, 5, 9, 10, 11, 12, 13, 14, 15, 16, 17]
+    units = [units[i] for i in turn]
+
+    send(0, kv_ref, block(0, 0, 0, c), core)
+    send(1, kv_ref, block(0, 0, 0, c), opposite)
+    send_y(0)
 
     for h in range(heads):
-        qa[h, :, 0:HD] = q_ref[:, h * HD : (h + 1) * HD]
-        qa[h, :, HD : 2 * HD] = qseg_ref[...]
-        m_ref[h] = jnp.full((BLK, HD), NEGATIVE, jnp.float32)
-        l_ref[h] = jnp.zeros((BLK, HD), jnp.float32)
-        acc_ref[h] = jnp.zeros((BLK, HD), jnp.float32)
-
+        qa[h * BLK : (h + 1) * BLK, 0:HD] = q_ref[:, h * HD : (h + 1) * HD]
+        qa[h * BLK : (h + 1) * BLK, HD : 2 * HD] = qseg_ref[...]
+    m_ref[...] = jnp.full_like(m_ref, NEGATIVE)
+    l_ref[...] = jnp.zeros_like(l_ref)
+    acc_ref[...] = jnp.zeros_like(acc_ref)
     low = bounds_ref[0:1, :]
     high = bounds_ref[1:2, :]
     quad_first = (me.y * 4 + x) * 4 * BLK
-    token = me.s * BLK + lax.broadcasted_iota(jnp.int32, (BLK, 1), 0)
-
-    def fold(blocks, first_key, causal):
-        count = len(blocks) * BLK
-        for i, block in enumerate(blocks):
-            rows = pl.ds(i * BLK, BLK)
-            kaug[rows, 0:HD] = block[:, 0:HD]
-            key = first_key + i * BLK + lax.broadcasted_iota(jnp.int32, (BLK, HD), 0)
-            inside = (key >= low) & (key < high)
-            kaug[rows, HD : 2 * HD] = jnp.where(inside, 0.0, NEGATIVE).astype(jnp.bfloat16)
-        values = jnp.concatenate([block[:, HD : 2 * HD] for block in blocks], axis=0)
-        key_row = first_key + lax.broadcasted_iota(jnp.int32, (1, count), 1)
-
-        def one_head(h, carry):
-            scores = lax.dot_general(
-                qa[h],
-                kaug[0:count, :],
-                (((1,), (1,)), ((), ())),
-                preferred_element_type=jnp.float32,
-            )
-            if causal:
-                scores = jnp.where(key_row <= token, scores, NEGATIVE)
-            old = m_ref[h]
-            new = jnp.maximum(old, jnp.max(scores, axis=1, keepdims=True))
-            weights = jnp.exp2(scores * scale2 - new[:, 0:1] * scale2)
-            factor = jnp.exp2((old - new) * scale2)
-            m_ref[h] = new
-            l_ref[h] = l_ref[h] * factor + jnp.sum(weights, axis=1, keepdims=True)
-            update = jnp.dot(
-                weights.astype(jnp.bfloat16), values, preferred_element_type=jnp.float32
-            )
-            acc_ref[h] = acc_ref[h] * factor + update
-            return carry
-
-        lax.fori_loop(0, heads, one_head, 0, unroll=2)
-
-    def quad(rx, k):
-        return [buf.at[rx, k, zz, cc] for zz in range(2) for cc in range(2)]
-
-    arrived(0, buf.at[0, 0, z, 1 - c])
-    fold([buf.at[0, 0, z, 0], buf.at[0, 0, z, 1]], quad_first + z * 2 * BLK, True)
-
-    arrived(1, buf.at[0, 0, 1 - z, c])
-    mine = lambda rx, k: buf.at[rx, k, :, c]
-    send(2, buf.at[0, 0, 1 - z, c], buf.at[0, 0, 1 - z, c], core)
-    send(3, mine(0, 0), mine(0, 1), me.at(dy=1))
-    send(4, mine(0, 0), mine(0, 2), me.at(dy=2))
-    arrived(2, buf.at[0, 0, 1 - z, 1 - c])
-    fold([buf.at[0, 0, 1 - z, 0], buf.at[0, 0, 1 - z, 1]], quad_first + (1 - z) * 2 * BLK, True)
-
-    order = (1, 3, 2)
-    other = lambda rx, k: buf.at[rx, k, :, 1 - c]
-    out_wrap = {rx: lax.div(x + rx, 4) for rx in order}
-    in_wrap = {rx: jnp.where(x < rx, 1, 0) for rx in order}
-
-    arrived(3, mine(0, 1))
-    send(5, mine(0, 1), mine(0, 1), core)
-    for rx in order:
-        send(6 + rx, mine(0, 1), mine(rx, 1 - out_wrap[rx]), me.at(dx=rx))
-    arrived(4, mine(0, 2))
-    send(6, mine(0, 2), mine(0, 2), core)
-    for rx in order:
-        send(9 + rx, mine(0, 2 * out_wrap[rx]), mine(rx, out_wrap[rx]), me.at(dx=rx))
-    arrived(5, other(0, 1))
-    fold(quad(0, 1), quad_first - 16 * BLK, False)
-    arrived(6, other(0, 2))
-    fold(quad(0, 2), quad_first - 32 * BLK, False)
-
-    stages = [(6 + rx, 12 + rx, rx, 1 - in_wrap[rx]) for rx in order]
-    stages += [(9 + rx, 15 + rx, rx, in_wrap[rx]) for rx in order]
-
-    def forward(stage):
-        first, second, rx, k = stage
-        arrived(first, mine(rx, k))
-        send(second, mine(rx, k), mine(rx, k), core)
-
-    forward(stages[0])
-    for i, (first, second, rx, k) in enumerate(stages):
-        if i + 1 < len(stages):
-            forward(stages[i + 1])
-        arrived(second, other(rx, k))
-        fold(quad(rx, k), quad_first - (rx + 4 * k) * 4 * BLK, False)
+    place = 2 * z + c
+
+    def step(source, first_key, causal):
+        key = first_key + lax.broadcasted_iota(jnp.int32, (BLK, HD), 0)
+        inside = (key >= low) & (key < high)
+        bias = jnp.where(inside, 0.0, NEGATIVE).astype(jnp.bfloat16)
+        keys = jnp.concatenate([source[:, 0:HD], bias], axis=1)
+        scores = lax.dot_general(
+            qa[...], keys, (((1,), (1,)), ((), ())), preferred_element_type=jnp.float32
+        )
+        if causal:
+            row = lax.broadcasted_iota(jnp.int32, scores.shape, 0) & (BLK - 1)
+            column = lax.broadcasted_iota(jnp.int32, scores.shape, 1)
+            scores = jnp.where(column <= row, scores, NEGATIVE)
+        old = m_ref[...]
+        new = jnp.maximum(old, jnp.max(scores, axis=1, keepdims=True))
+        offset = new * scale2
+        weights = jnp.exp2(scores * scale2 - jnp.concatenate([offset, offset], axis=1))
+        factor = jnp.exp2((old - new) * scale2)
+        m_ref[...] = new
+        l_ref[...] = l_ref[...] * factor + (weights[:, 0:HD] + weights[:, HD : 2 * HD])
+        update = jnp.dot(
+            weights.astype(jnp.bfloat16), source[:, HD : 2 * HD], preferred_element_type=jnp.float32
+        )
+        acc_ref[...] = acc_ref[...] * factor + update
+
+    step(block(0, 0, 0, c), quad_first + place * BLK, True)
+
+    def chosen(n, field):
+        value = 0
+        for i, unit in enumerate(units):
+            value = value + (n == i).astype(jnp.int32) * unit[field]
+        return value
+
+    def serve(i):
+        rx, k, zi, first, then = units[i]
+        forward(first, then, rx, k, zi)
+        if (rx, k) == (0, 1):
+            send_first(zi)
+        if (rx, k) == (0, 2):
+            send_second(zi, 1)
+        if (rx, k) == (0, 0):
+            send_y(1)
+
+    def one_unit(n, carry):
+        for i in range(1, len(units)):
+
+            @pl.when(n == i - 1)
+            def _():
+                serve(i)
+
+        rx, k, zi, then = (chosen(n, field) for field in (0, 1, 2, 4))
+
+        @pl.when(n < 8)
+        def _():
+            for i in range(8):
+
+                @pl.when(n * 8 + i > 0)
+                def _():
+                    to = peer(n * 8 + i)
+                    remote(pages_ref.at[to[0]], pages.at[me.s], ss.at[35], rs.at[35], to).start()
+
+        def one_core(j, inner):
+            cc = wrap(c + j, 2)
+            source = block(rx, k, zi, cc)
+            where = 2 * wrap(z + zi, 2) + cc
+
+            @pl.when(j == 1)
+            def _():
+                arrived(then, source)
+
+            distance = rx + 4 * k
+            first_key = quad_first - distance * 4 * BLK + where * BLK
+            skip = ((distance == 0) & (where >= place)) | ((distance == 8) & (where < place))
+
+            @pl.when(jnp.logical_not(skip) & (first_key >= 0))
+            def _():
+                step(source, first_key, False)
+
+            return inner
+
+        return lax.fori_loop(0, 2, one_core, carry)
+
+    lax.fori_loop(0, len(units), one_unit, 0)
 
     for h in range(heads):
-        out_ref[:, h * HD : (h + 1) * HD] = (acc_ref[h] / l_ref[h]).astype(out_ref.dtype)
-    for copy in started:
-        copy.wait_send()
-
-
-def attend(kv_block, queries, query_onehot, bounds):
+        rows = slice(h * BLK, (h + 1) * BLK)
+        total = jnp.sum(l_ref[rows, :], axis=1, keepdims=True)
+        out_ref[:, h * HD : (h + 1) * HD] = (acc_ref[rows, :] / total).astype(out_ref.dtype)
+
+    others = pl.ds(0, owners - 1)
+    exchange = remote(pages_ref.at[others], pages.at[others], ss.at[35], rs.at[35], core)
+    exchange.wait_recv()
+    cache_ref[...] = pages[...]
+    exchange.wait_send()
+    for index in range(35):
+        remote(kv_ref, block(0, 0, 0, c), ss.at[index], rs.at[index], core).wait_send()
+
+
+def attend(kv_block, queries, query_onehot, bounds, outgoing):
     heads = queries.shape[1] // HD
     vmem = pl.BlockSpec(memory_space=pltpu.VMEM)
     return pl.pallas_call(
         attend_kernel,
-        out_shape=jax.ShapeDtypeStruct(queries.shape, jnp.bfloat16),
-        in_specs=[vmem] * 4,
-        out_specs=vmem,
+        out_shape=(
+            jax.ShapeDtypeStruct(queries.shape, jnp.bfloat16),
+            jax.ShapeDtypeStruct(outgoing.shape, jnp.bfloat16),
+        ),
+        in_specs=[vmem] * 5,
+        out_specs=(vmem, vmem),
         scratch_shapes=[
             pltpu.VMEM((4, 3, 2, 2, BLK, 2 * HD), jnp.bfloat16),
-            pltpu.VMEM((heads, BLK, 2 * HD), jnp.bfloat16),
-            pltpu.VMEM((4 * BLK, 2 * HD), jnp.bfloat16),
-            pltpu.VMEM((heads, BLK, HD), jnp.float32),
-            pltpu.VMEM((heads, BLK, HD), jnp.float32),
-            pltpu.VMEM((heads, BLK, HD), jnp.float32),
-            pltpu.SemaphoreType.DMA((19,)),
-            pltpu.SemaphoreType.DMA((19,)),
+            pltpu.VMEM(outgoing.shape, jnp.bfloat16),
+            pltpu.VMEM((heads * BLK, 2 * HD), jnp.bfloat16),
+            pltpu.VMEM((heads * BLK, HD), jnp.float32),
+            pltpu.VMEM((heads * BLK, HD), jnp.float32),
+            pltpu.VMEM((heads * BLK, HD), jnp.float32),
+            pltpu.SemaphoreType.DMA((36,)),
+            pltpu.SemaphoreType.DMA((36,)),
         ],
         compiler_params=pltpu.CompilerParams(
             collective_id=0, has_side_effects=True, vmem_limit_bytes=48 << 20
@@ -436,7 +510,7 @@
         cost_estimate=pl.CostEstimate(
             flops=9_000_000_000, bytes_accessed=2_000_000, transcendentals=17_000_000
         ),
-    )(kv_block, queries, query_onehot, bounds)
+    )(kv_block, queries, query_onehot, bounds, outgoing)
 
 
 def on_device(hidden, norm_gain, kv_weight, queries, segment_ids, page_owner):
@@ -461,7 +535,6 @@
     low = jnp.full((HD,), stream_rows, jnp.int32).at[:SEGS].set(starts)
     high = jnp.full((HD,), stream_rows, jnp.int32).at[: SEGS - 1].set(starts[1:])
     bounds = jnp.zeros((8, HD), jnp.int32).at[0].set(low).at[1].set(high)
-    attended = attend(kv_block, queries, query_onehot, bounds)
 
     pages_block = page_owner.shape[0]
     page_rows = block_rows // pages_block
@@ -477,8 +550,8 @@
     columns_dev = kv_block.shape[1]
     pages = kv_block.reshape(pages_block, page_rows * columns_dev)
     outgoing = jnp.dot(select, pages, preferred_element_type=jnp.float32).astype(jnp.bfloat16)
-    outgoing = outgoing.reshape(seq_count, capacity, page_rows, columns_dev)
-    arrived = lax.all_to_all(outgoing, "seq", split_axis=0, concat_axis=0, tiled=True)
+    outgoing = outgoing.reshape(seq_count, capacity * page_rows * columns_dev // HD, HD)
+    attended, arrived = attend(kv_block, queries, query_onehot, bounds, outgoing)
     kv_cache = arrived.reshape(1, seq_count, capacity, page_rows, columns_dev)
     return (attended, kv_cache)
 

time: 157 us -> 123 us (0.78)
  the two profiles are of different devices: /device:TPU:1 before, /device:TPU:25 now
where the time goes in v3:
time: 123 us
  Pallas kernels  115 us (93%)
  local copies, waits for them, and re-layouts  4.31 us (4%)
  other arithmetic  2.86 us (2%)
    pallas_call x1, Pallas kernels, project(): pl.pallas_call(project_kernel, out_shape=(jax.ShapeDtypeStruct((4 * rows,...  57.7 us
    pallas_call x1, Pallas kernels, attend(): pl.pallas_call(attend_kernel, out_shape=(jax.ShapeDtypeStruct(queries.sha...  57 us
    unnamed x12, local copies, waits for them, and re-layouts  2.75 us

profile of v3, /device:TPU:25, one launch (start us, length us, event | category | flops | bytes accessed | tf_op | source)
XLA Modules:
  0.0 122.9 jit_solution(11729236228125630727)
XLA Ops:
  0.6 0.0 copy-start.3
  0.6 0.0 copy-start.4
  0.7 0.9 convert_reduce_fusion
  1.6 0.0 copy-start.2
  1.6 0.7 multiply_add_fusion
  2.3 0.0 copy-done.4
  2.3 0.1 select_reduce_fusion.1
  2.4 0.0 copy-done.3
  2.5 0.1 fusion.6.qseg_ref
  2.6 0.0 copy-done.2
  2.6 0.0 copy-start
  2.6 1.2 copy-done
  3.8 57.7 %shard_map.77 = (f32[256,256]{1,0:T(8,128)S(1)}, s32[8,128]{1,0:T(8,128)S(1)}) custom-call(bf16[64,8192]{1,0:T(8,128)(2,1)S(1)} %copy-done, bf16[1,8192]{1,0:T(2,128)(2,1)S(1)} %broadcast_in_dim.30.gain_ref, bf16[128,256]{1,0:T(8,128)(2,1)S(1)} %copy-done.2, s32[8,128]{1,0:T(8,128)S(1)} %broadcast_in_dim.33.first_ref), custom_call_target="tpu_custom_call" | custom-call | flops 1100000000 | bytes 2000000 | tf_op jit(solution)/shard_map/pallas_call | solution.py:263
  61.5 0.1 reshape.220
  61.7 0.1 slice.76
  61.8 0.1 select_reduce_fusion
  61.9 0.1 slice.80
  62.0 0.1 slice.77
  62.1 0.6 fusion.4
  62.7 0.1 pad_maximum_fusion
  62.8 0.3 maximum_convert_fusion
  63.1 0.1 convert_element_type.29
  63.2 0.0 copy-start.1
  63.2 0.2 convolution_convert_fusion
  63.4 0.1 reshape.221.pages_ref
  63.5 0.7 copy-done.1
  64.2 57.0 %shard_map.78 = (bf16[256,1024]{1,0:T(8,128)(2,1)S(1)}, bf16[64,16,128]{2,1,0:T(8,128)(2,1)S(1)}) custom-call(bf16[256,256]{1,0:T(8,128)(2,1)S(1)} %bitcast.17, bf16[256,1024]{1,0:T(8,128)(2,1)S(1)} %copy-done.1, bf16[256,128]{1,0:T(8,128)(2,1)S(1)} %fusion.6.qseg_ref, s32[8,128]{1,0:T(8,128)S(1)} %scatter.19.bounds_ref, ...), custom_call_target="tpu_custom_call" | custom-call | flops 8999999488 | bytes 2000000 | tf_op jit(solution)/shard_map/pallas_call | solution.py:489
  121.3 0.9 reshape.222
  122.1 0.8 copy.15
  (11 shorter events, 0.1 us)
Async XLA Ops:
  0.6 1.8 %copy-start.3 = (bf16[8192]{0:T(1024)(128)(2,1)S(1)}, bf16[8192]{0:T(1024)(128)(2,1)}, u32[]{:S(2)}) copy-start(bf16[8192]{0:T(1024)(128)(2,1)} %param.15) | copy-start | bytes 49156
  0.6 1.6 %copy-start.4 = (s32[256]{0:T(256)S(1)}, s32[256]{0:T(256)}, u32[]{:S(2)}) copy-start(s32[256]{0:T(256)} %param.18) | copy-start | bytes 3076
  1.6 1.0 copy-start.2
  2.6 1.2 copy-start
  63.2 1.0 copy-start.1

commit v4 on v3

--- a/solution.py
+++ b/solution.py
@@ -14,26 +14,6 @@
 LOG2E = 1.4426950408889634
 MESH = pl.DeviceIdType.MESH
 BLK = 256
-
-
-def rotate_keys(keys, positions):
-    half = keys.shape[-1] // 2
-    freq = 10000.0 ** (-jnp.arange(half, dtype=jnp.float32) * 2.0 / keys.shape[-1])
-    angle = positions.astype(jnp.float32)[:, None] * freq[None, :]
-    cosine = jnp.cos(angle)[:, None, :]
-    sine = jnp.sin(angle)[:, None, :]
-    first = keys[..., :half]
-    second = keys[..., half:]
-    return jnp.concatenate(
-        [first * cosine - second * sine, second * cosine + first * sine], axis=-1
-    )
-
-
-def pair_keys(projected, positions, head_size):
-    rows = projected.shape[0]
-    pairs = projected.reshape(rows, -1, 2, head_size)
-    turned = rotate_keys(pairs[:, :, 0], positions)
-    return jnp.stack([turned, pairs[:, :, 1]], axis=2).reshape(rows, -1).astype(jnp.bfloat16)
 
 
 def wrap(value, count):
@@ -64,10 +44,7 @@
     )
 
 
-def project_kernel(
-    hid_ref, gain_ref, w_ref, first_ref, out_ref, starts_ref, nb, wb, fb, acc, res, got, ss, rs
-):
-    me = Place()
+def project_part(me, hid_ref, gain_ref, w_ref, first_ref, nb, wb, fb, acc, res, got, ss, rs, enter):
     c, z, x, y, f = me.c, me.z, me.x, me.y, me.f
     parity, group = lax.rem(f, 2), lax.div(f, 2)
     head = parity + 2 * c
@@ -82,12 +59,7 @@
     core = near(z, 1 - c, f)
     ring_x = {k: me.at(dx=k) for k in (1, 2, 3)}
     ring_y = {k: me.at(dy=k) for k in (1, 2, 3)}
-    cube = [near(zz, cc, ff) for ff in (f, twin) for zz in (z, 1 - z) for cc in (c, 1 - c)][1:]
-    partners = cube + [near(z, c, mate)] + list(ring_x.values()) + list(ring_y.values())
-    barrier = pltpu.get_barrier_semaphore()
-    for partner in partners:
-        pl.semaphore_signal(barrier, inc=1, device_id=partner, device_id_type=MESH)
-    pl.semaphore_wait(barrier, len(partners))
+    enter([near(zz, cc, twin) for zz in (z, 1 - z) for cc in (c, 1 - c)] + [near(z, c, mate)])
 
     started = []
 
@@ -194,7 +166,7 @@
     forward(3)
     for k in order:
         arrived(9 + k, fb.at[7 + k])
-    starts_ref[...] = jnp.minimum(jnp.minimum(fb[7], fb[8]), jnp.minimum(fb[9], fb[10]))
+    fb[11] = jnp.minimum(jnp.minimum(fb[7], fb[8]), jnp.minimum(fb[9], fb[10]))
     for i in range(chunks):
         arrived(17 + i, nb.at[1 - c, parity, i])
         arrived(21 + i, nb.at[1 - c, 1 - parity, i])
@@ -241,55 +213,29 @@
         def _():
             arrived(55 + g, got.at[g])
 
-    out_ref[...] = got[...].reshape(out_ref.shape)
-    for copy in started:
-        copy.wait_send()
-
-    @pl.when(home)
-    def _():
-        result_to(1 - c, f, 55).wait_send()
-
-    @pl.when(jnp.logical_not(home))
-    def _():
-        seed_to_core().wait_send()
-        result_to(0, twin, 55).wait_send()
-        result_to(1, twin, 56).wait_send()
-
-
-def project(hidden, gain, weight, firsts):
-    rows, width = hidden.shape
-    columns = weight.shape[1]
-    vmem = pl.BlockSpec(memory_space=pltpu.VMEM)
-    return pl.pallas_call(
-        project_kernel,
-        out_shape=(
-            jax.ShapeDtypeStruct((4 * rows, columns), jnp.float32),
-            jax.ShapeDtypeStruct((8, HD), jnp.int32),
-        ),
-        in_specs=[vmem] * 4,
-        out_specs=(vmem, vmem),
-        scratch_shapes=[
-            pltpu.VMEM((2, 2, 4, rows, width // 4), jnp.bfloat16),
-            pltpu.VMEM((16, 2, width // 32, columns), jnp.bfloat16),
-            pltpu.VMEM((11, 8, HD), jnp.int32),
-            pltpu.VMEM((4 * rows, columns), jnp.float32),
-            pltpu.VMEM((2, 2 * rows, columns), jnp.float32),
-            pltpu.VMEM((2, 2 * rows, columns), jnp.float32),
-            pltpu.SemaphoreType.DMA((57,)),
-            pltpu.SemaphoreType.DMA((57,)),
-        ],
-        compiler_params=pltpu.CompilerParams(
-            collective_id=1, has_side_effects=True, vmem_limit_bytes=48 << 20
-        ),
-        cost_estimate=pl.CostEstimate(
-            flops=1_100_000_000, bytes_accessed=2_000_000, transcendentals=0
-        ),
-    )(hidden, gain, weight, firsts)
-
-
-def attend_kernel(
-    kv_ref, q_ref, qseg_ref, bounds_ref, pages_ref, out_ref, cache_ref,
-    buf, pages, qa, m_ref, l_ref, acc_ref, ss, rs
+
+    def finish():
+        for copy in started:
+            copy.wait_send()
+
+        @pl.when(home)
+        def _():
+            result_to(1 - c, f, 55).wait_send()
+
+        @pl.when(jnp.logical_not(home))
+        def _():
+            seed_to_core().wait_send()
+            result_to(0, twin, 55).wait_send()
+            result_to(1, twin, 56).wait_send()
+
+    return finish
+
+
+def layer_kernel(
+    hid_ref, gain_ref, w_ref, first_ref, q_ref, qseg_ref, freq_ref, target_ref,
+    out_ref, cache_ref,
+    nb, wb, fb, proj, res, got, ass, ars,
+    buf, pages, pages_ref, qa, m_ref, l_ref, acc_ref, ss, rs
 ):
     me = Place()
     c, z, x = me.c, me.z, me.x
@@ -302,16 +248,46 @@
     def peer(distance):
         return (wrap(me.s + distance, owners), me.f)
 
-    barrier = pltpu.get_barrier_semaphore()
-
-    def greet(distance, carry):
-        pl.semaphore_signal(barrier, inc=1, device_id=peer(distance), device_id_type=MESH)
-        return carry
-
-    lax.fori_loop(1, owners, greet, 0)
-    buf[0, 0, z, c] = kv_ref[...]
-    pages[me.s] = pages_ref[me.s]
-    pl.semaphore_wait(barrier, owners - 1)
+    def enter(others):
+        barrier = pltpu.get_barrier_semaphore()
+
+        def greet(distance, carry):
+            pl.semaphore_signal(barrier, inc=1, device_id=peer(distance), device_id_type=MESH)
+            return carry
+
+        for other in others:
+            pl.semaphore_signal(barrier, inc=1, device_id=other, device_id_type=MESH)
+        lax.fori_loop(1, owners, greet, 0)
+        for h in range(heads):
+            qa[h * BLK : (h + 1) * BLK, 0:HD] = q_ref[:, h * HD : (h + 1) * HD]
+            qa[h * BLK : (h + 1) * BLK, HD : 2 * HD] = qseg_ref[...]
+        m_ref[...] = jnp.full_like(m_ref, NEGATIVE)
+        l_ref[...] = jnp.zeros_like(l_ref)
+        acc_ref[...] = jnp.zeros_like(acc_ref)
+        pl.semaphore_wait(barrier, owners - 1 + len(others))
+
+    finish = project_part(
+        me, hid_ref, gain_ref, w_ref, first_ref, nb, wb, fb, proj, res, got, ass, ars, enter
+    )
+
+    bounds = fb[11]
+    low = bounds[0:1, :]
+    high = bounds[1:2, :]
+    begin = jnp.sum(
+        qseg_ref[...].astype(jnp.float32) * low.astype(jnp.float32), axis=1, keepdims=True
+    )
+    token = (me.s * BLK + lax.broadcasted_iota(jnp.int32, (BLK, HD), 0)).astype(jnp.float32)
+    angle = (token - begin) * freq_ref[0:1, :]
+    lane = lax.broadcasted_iota(jnp.int32, (BLK, HD), 1)
+    sine = jnp.sin(angle)
+    sine = jnp.where(lane < HD // 2, -sine, sine)
+    projected = got[...].reshape(BLK, 2 * HD)
+    keys = projected[:, 0:HD]
+    swapped = jnp.concatenate([keys[:, HD // 2 :], keys[:, : HD // 2]], axis=1)
+    turned = keys * jnp.cos(angle) + swapped * sine
+    kv = jnp.concatenate([turned, projected[:, HD:]], axis=1).astype(jnp.bfloat16)
+    kv_ref = buf.at[0, 0, z, c]
+    kv_ref[...] = kv
 
     def send(index, src, dst, target):
         remote(src, dst, ss.at[index], rs.at[index], target).start()
@@ -375,14 +351,12 @@
     send(1, kv_ref, block(0, 0, 0, c), opposite)
     send_y(0)
 
-    for h in range(heads):
-        qa[h * BLK : (h + 1) * BLK, 0:HD] = q_ref[:, h * HD : (h + 1) * HD]
-        qa[h * BLK : (h + 1) * BLK, HD : 2 * HD] = qseg_ref[...]
-    m_ref[...] = jnp.full_like(m_ref, NEGATIVE)
-    l_ref[...] = jnp.zeros_like(l_ref)
-    acc_ref[...] = jnp.zeros_like(acc_ref)
-    low = bounds_ref[0:1, :]
-    high = bounds_ref[1:2, :]
+    row = lax.broadcasted_iota(jnp.int32, (owners * 8, BLK), 0)
+    select = (row == target_ref[0:1, :]).astype(jnp.bfloat16)
+    chosen_pages = jnp.dot(select, kv, preferred_element_type=jnp.float32)
+    pages_ref[...] = chosen_pages.astype(jnp.bfloat16).reshape(pages_ref.shape)
+    pages[me.s] = pages_ref[me.s]
+
     quad_first = (me.y * 4 + x) * 4 * BLK
     place = 2 * z + c
 
@@ -481,22 +455,35 @@
     exchange.wait_send()
     for index in range(35):
         remote(kv_ref, block(0, 0, 0, c), ss.at[index], rs.at[index], core).wait_send()
-
-
-def attend(kv_block, queries, query_onehot, bounds, outgoing):
+    finish()
+
+
+def layer(hidden, gain, weight, firsts, queries, query_onehot, freq, target):
     heads = queries.shape[1] // HD
+    rows, width = hidden.shape
+    columns = weight.shape[1]
+    owners = lax.axis_size("seq")
     vmem = pl.BlockSpec(memory_space=pltpu.VMEM)
     return pl.pallas_call(
-        attend_kernel,
+        layer_kernel,
         out_shape=(
             jax.ShapeDtypeStruct(queries.shape, jnp.bfloat16),
-            jax.ShapeDtypeStruct(outgoing.shape, jnp.bfloat16),
+            jax.ShapeDtypeStruct((owners, 8, columns), jnp.bfloat16),
         ),
-        in_specs=[vmem] * 5,
+        in_specs=[vmem] * 8,
         out_specs=(vmem, vmem),
         scratch_shapes=[
+            pltpu.VMEM((2, 2, 4, rows, width // 4), jnp.bfloat16),
+            pltpu.VMEM((16, 2, width // 32, columns), jnp.bfloat16),
+            pltpu.VMEM((12, 8, HD), jnp.int32),
+            pltpu.VMEM((4 * rows, columns), jnp.float32),
+            pltpu.VMEM((2, 2 * rows, columns), jnp.float32),
+            pltpu.VMEM((2, 2 * rows, columns), jnp.float32),
+            pltpu.SemaphoreType.DMA((57,)),
+            pltpu.SemaphoreType.DMA((57,)),
             pltpu.VMEM((4, 3, 2, 2, BLK, 2 * HD), jnp.bfloat16),
-            pltpu.VMEM(outgoing.shape, jnp.bfloat16),
+            pltpu.VMEM((owners, 8, columns), jnp.bfloat16),
+            pltpu.VMEM((owners, 8, columns), jnp.bfloat16),
             pltpu.VMEM((heads * BLK, 2 * HD), jnp.bfloat16),
             pltpu.VMEM((heads * BLK, HD), jnp.float32),
             pltpu.VMEM((heads * BLK, HD), jnp.float32),
@@ -505,12 +492,12 @@
             pltpu.SemaphoreType.DMA((36,)),
         ],
         compiler_params=pltpu.CompilerParams(
-            collective_id=0, has_side_effects=True, vmem_limit_bytes=48 << 20
+            collective_id=0, has_side_effects=True, vmem_limit_bytes=52 << 20
         ),
         cost_estimate=pl.CostEstimate(
-            flops=9_000_000_000, bytes_accessed=2_000_000, transcendentals=17_000_000
+            flops=10_000_000_000, bytes_accessed=4_000_000, transcendentals=17_000_000
         ),
-    )(kv_block, queries, query_onehot, bounds, outgoing)
+    )(hidden, gain, weight, firsts, queries, query_onehot, freq, target)
 
 
 def on_device(hidden, norm_gain, kv_weight, queries, segment_ids, page_owner):
@@ -518,23 +505,15 @@
     seq_place = lax.axis_index("seq")
     block_rows = segment_ids.shape[0]
     stream_rows = block_rows * seq_count
-    anchor = seq_place * block_rows
-    token_index = anchor + jnp.arange(block_rows, dtype=jnp.int32)
-    labels = jnp.arange(SEGS, dtype=jnp.int32)
-    member = segment_ids[:, None] == labels[None, :]
-    firsts = jnp.min(jnp.where(member, token_index[:, None], stream_rows), axis=0)
-    first_tile = jnp.broadcast_to(jnp.pad(firsts, (0, HD - SEGS))[None, :], (8, HD))
-    projected, start_tile = project(hidden, norm_gain[None, :], kv_weight, first_tile)
-    starts = start_tile[0, :SEGS]
-    query_start = jnp.sum(jnp.where(member, starts[None, :], 0), axis=1)
-    positions = token_index - query_start
-    kv_block = pair_keys(projected, positions, HD)
-
+    token_index = seq_place * block_rows + jnp.arange(block_rows, dtype=jnp.int32)
     lanes = jnp.arange(HD, dtype=jnp.int32)
-    query_onehot = (segment_ids[:, None] == lanes[None, :]).astype(jnp.bfloat16)
-    low = jnp.full((HD,), stream_rows, jnp.int32).at[:SEGS].set(starts)
-    high = jnp.full((HD,), stream_rows, jnp.int32).at[: SEGS - 1].set(starts[1:])
-    bounds = jnp.zeros((8, HD), jnp.int32).at[0].set(low).at[1].set(high)
+    member = segment_ids[:, None] == lanes[None, :]
+    wanted = jnp.stack([lanes, lanes + 1])
+    hit = segment_ids[None, None, :] == wanted[:, :, None]
+    firsts = jnp.min(jnp.where(hit, token_index[None, None, :], stream_rows), axis=2)
+    first_tile = jnp.pad(firsts, ((0, 6), (0, 0)))
+    freq = 10000.0 ** (-jnp.arange(HD // 2, dtype=jnp.float32) * 2.0 / HD)
+    freq_tile = jnp.broadcast_to(jnp.concatenate([freq, freq])[None, :], (8, HD))
 
     pages_block = page_owner.shape[0]
     page_rows = block_rows // pages_block
@@ -543,16 +522,21 @@
     order = jnp.arange(pages_block, dtype=jnp.int32)
     earlier = (owners[None, :] == owners[:, None]) & (order[None, :] < order[:, None])
     rank = jnp.sum(earlier.astype(jnp.int32), axis=1)
-    target = owners * capacity + rank
-    select = (jnp.arange(seq_count * capacity, dtype=jnp.int32)[:, None] == target[None, :]).astype(
-        jnp.bfloat16
+    slot = (owners * capacity + rank) * page_rows
+    target = (slot[:, None] + jnp.arange(page_rows, dtype=jnp.int32)[None, :]).reshape(1, block_rows)
+    target_tile = jnp.broadcast_to(target, (8, block_rows))
+
+    attended, arrived = layer(
+        hidden,
+        norm_gain[None, :],
+        kv_weight,
+        first_tile,
+        queries,
+        member.astype(jnp.bfloat16),
+        freq_tile,
+        target_tile,
     )
-    columns_dev = kv_block.shape[1]
-    pages = kv_block.reshape(pages_block, page_rows * columns_dev)
-    outgoing = jnp.dot(select, pages, preferred_element_type=jnp.float32).astype(jnp.bfloat16)
-    outgoing = outgoing.reshape(seq_count, capacity * page_rows * columns_dev // HD, HD)
-    attended, arrived = attend(kv_block, queries, query_onehot, bounds, outgoing)
-    kv_cache = arrived.reshape(1, seq_count, capacity, page_rows, columns_dev)
+    kv_cache = arrived.reshape(1, seq_count, capacity, page_rows, arrived.shape[2])
     return (attended, kv_cache)
 
 

time: 123 us -> 117 us (0.951)
  the two profiles are of different devices: /device:TPU:25 before, /device:TPU:57 now
where the time goes in v4:
time: 117 us
  Pallas kernels  111 us (95%)
  local copies, waits for them, and re-layouts  4.76 us (4%)
    pallas_call x1, Pallas kernels, layer(): pl.pallas_call(layer_kernel, out_shape=(jax.ShapeDtypeStruct(queries.shap...  111 us
    unnamed x11, local copies, waits for them, and re-layouts  3.85 us

profile of v4, /device:TPU:57, one launch (start us, length us, event | category | flops | bytes accessed | tf_op | source)
XLA Modules:
  0.0 116.8 jit_solution(13968160209944307326)
XLA Ops:
  0.6 0.0 copy-start.4
  0.6 0.6 copy-done.4
  1.3 0.2 convert_reduce_fusion
  1.5 0.1 pad_maximum_fusion
  1.6 0.0 copy-start.3
  1.6 0.7 copy-done.3
  2.3 0.2 select_reduce_fusion
  2.5 0.1 iota_add_fusion
  2.6 0.0 copy-start.2
  2.6 0.1 add.60
  2.7 0.0 copy-start.1
  2.7 0.6 copy-done.2
  3.3 0.1 fusion.qseg_ref
  3.4 0.1 copy-done.1
  3.5 0.0 copy-start
  3.5 1.0 copy-done
  4.6 110.7 %shard_map.77 = (bf16[256,1024]{1,0:T(8,128)(2,1)S(1)}, bf16[64,8,256]{2,1,0:T(8,128)(2,1)S(1)}) custom-call(bf16[64,8192]{1,0:T(8,128)(2,1)} %hid_ref.1, bf16[1,8192]{1,0:T(2,128)(2,1)S(1)} %broadcast_in_dim.18.gain_ref, bf16[128,256]{1,0:T(8,128)(2,1)S(1)} %copy-done.1, s32[8,128]{1,0:T(8,128)S(1)} %pad.4.first_ref, bf16[256,1024]{1,0:T(8,128)(2,1)S(1)} %copy-done, ...), custom_call_target="tpu_custom_call" | custom-call | flops 10000000000 | bytes 4000000 | tf_op jit(solution)/shard_map/pallas_call | solution.py:467
  115.3 0.8 reshape.39
  116.1 0.8 copy.9
  (10 shorter events, 0.1 us)
Async XLA Ops:
  0.6 0.7 copy-start.4
  1.6 0.7 copy-start.3
  2.6 0.7 copy-start.2
  2.7 0.8 copy-start.1
  3.5 1.0 copy-start

commit v5 on v4

--- a/solution.py
+++ b/solution.py
@@ -44,7 +44,10 @@
     )
 
 
-def project_part(me, hid_ref, gain_ref, w_ref, first_ref, nb, wb, fb, acc, res, got, ss, rs, enter):
+def project_part(
+    me, hid_ref, gain_ref, w_ref, first_ref, qseg_ref, freq_ref,
+    nb, wb, fb, acc, res, begins, buf, ss, rs, local, enter, idle
+):
     c, z, x, y, f = me.c, me.z, me.x, me.y, me.f
     parity, group = lax.rem(f, 2), lax.div(f, 2)
     head = parity + 2 * c
@@ -84,7 +87,7 @@
 
     @pl.when(home)
     def _():
-        wb[quad, z, pl.ds(pl.multiple_of(c * rows_w, rows_w), rows_w)] = w_ref[...]
+        pltpu.make_async_copy(w_ref, piece(z, c), local).start()
 
     @pl.when(jnp.logical_not(home))
     def _():
@@ -113,6 +116,10 @@
         for cc in (0, 1):
             own = jnp.logical_and(home, shard == 2 * zz + cc)
 
+            @pl.when(own)
+            def _():
+                pltpu.make_async_copy(w_ref, piece(zz, cc), local).wait()
+
             @pl.when(jnp.logical_not(own))
             def _():
                 arrived(2 * zz + cc, piece(zz, cc))
@@ -147,6 +154,7 @@
         send(21 + i, nb.at[c, 1 - parity, i], nb.at[c, 1 - parity, i], core)
 
     spread(0)
+    idle()
     for i in range(3):
         arrived(4 + i, fb.at[i])
     fb[3] = jnp.minimum(jnp.minimum(first_ref[...], fb[0]), jnp.minimum(fb[1], fb[2]))
@@ -167,6 +175,10 @@
     for k in order:
         arrived(9 + k, fb.at[7 + k])
     fb[11] = jnp.minimum(jnp.minimum(fb[7], fb[8]), jnp.minimum(fb[9], fb[10]))
+    first_row = fb[11][0:1, :].astype(jnp.float32)
+    begin = jnp.sum(qseg_ref[...].astype(jnp.float32) * first_row, axis=1, keepdims=True)
+    begins[c] = jnp.broadcast_to(begin, begins.shape[1:])
+    send(59, begins.at[c], begins.at[c], core)
     for i in range(chunks):
         arrived(17 + i, nb.at[1 - c, parity, i])
         arrived(21 + i, nb.at[1 - c, 1 - parity, i])
@@ -192,27 +204,53 @@
             arrived(b2(k, j), half(yy, xx, 1))
             multiply(yy, xx, 1)
 
-    res[...] = acc[...].reshape(res.shape)
-
-    def result_to(cc, ff, index):
-        return remote(res.at[cc], got.at[group], ss.at[index], rs.at[55 + group], near(z, cc, ff))
+    arrived(59, begins.at[1 - c])
+    pair = 2 * rows
+    rows_g = pl.ds(pl.multiple_of(group * pair, pair), pair)
+    lane = lax.broadcasted_iota(jnp.int32, (pair, HD), 1)
+    for cc in (0, 1):
+        first_token = (me.s - c + cc) * BLK + group * pair
+        token = first_token + lax.broadcasted_iota(jnp.int32, (pair, HD), 0)
+        angle = (token.astype(jnp.float32) - begins[cc, rows_g, :]) * freq_ref[0:1, :]
+        sine = jnp.sin(angle)
+        sine = jnp.where(lane < HD // 2, -sine, sine)
+        keys = acc[cc * pair : (cc + 1) * pair, 0:HD]
+        swapped = jnp.concatenate([keys[:, HD // 2 :], keys[:, : HD // 2]], axis=1)
+        turned = keys * jnp.cos(angle) + swapped * sine
+        res[cc, :, 0:HD] = turned.astype(jnp.bfloat16)
+        res[cc, :, HD:] = acc[cc * pair : (cc + 1) * pair, HD:].astype(jnp.bfloat16)
+
+    def part(zz, cc, g):
+        return buf.at[0, 0, zz, cc, pl.ds(pl.multiple_of(g * pair, pair), pair)]
+
+    def result_to(zz, cc, ff, index, recv):
+        return remote(
+            res.at[cc], part(z, cc, group), ss.at[index], rs.at[recv + group], near(zz, cc, ff)
+        )
 
     @pl.when(home)
     def _():
-        result_to(1 - c, f, 55).start()
-        got[group] = res[c]
+        result_to(z, 1 - c, f, 55, 55).start()
+        result_to(1 - z, 0, f, 57, 57).start()
+        result_to(1 - z, 1, f, 58, 57).start()
+        buf[0, 0, z, c, rows_g, :] = res[c]
 
     @pl.when(jnp.logical_not(home))
     def _():
-        result_to(0, twin, 55).start()
-        result_to(1, twin, 56).start()
+        result_to(z, 0, twin, 55, 55).start()
+        result_to(z, 1, twin, 56, 55).start()
+        result_to(1 - z, 0, twin, 57, 57).start()
+        result_to(1 - z, 1, twin, 58, 57).start()
 
     for g in (0, 1):
 
         @pl.when(jnp.logical_not(jnp.logical_and(home, group == g)))
         def _():
-            arrived(55 + g, got.at[g])
-
+            arrived(55 + g, part(z, c, g))
+
+    def opposite_arrived():
+        for g in (0, 1):
+            arrived(57 + g, part(1 - z, c, g))
 
     def finish():
         for copy in started:
@@ -220,30 +258,36 @@
 
         @pl.when(home)
         def _():
-            result_to(1 - c, f, 55).wait_send()
+            result_to(z, 1 - c, f, 55, 55).wait_send()
 
         @pl.when(jnp.logical_not(home))
         def _():
             seed_to_core().wait_send()
-            result_to(0, twin, 55).wait_send()
-            result_to(1, twin, 56).wait_send()
-
-    return finish
+            result_to(z, 0, twin, 55, 55).wait_send()
+            result_to(z, 1, twin, 56, 55).wait_send()
+
+        result_to(1 - z, 0, f, 57, 57).wait_send()
+        result_to(1 - z, 1, f, 58, 57).wait_send()
+
+    return finish, opposite_arrived
 
 
 def layer_kernel(
-    hid_ref, gain_ref, w_ref, first_ref, q_ref, qseg_ref, freq_ref, target_ref,
+    hid_hbm, gain_ref, w_ref, first_ref, q_hbm, qseg_ref, freq_ref, target_ref,
     out_ref, cache_ref,
-    nb, wb, fb, proj, res, got, ass, ars,
+    hid, q, nb, wb, fb, proj, res, begins, ass, ars, local,
     buf, pages, pages_ref, qa, m_ref, l_ref, acc_ref, ss, rs
 ):
     me = Place()
     c, z, x = me.c, me.z, me.x
-    heads = q_ref.shape[1] // HD
+    heads = q.shape[1] // HD
     owners = pages_ref.shape[0]
     scale2 = (HD ** (-0.5)) * LOG2E
     core = me.at(other_core=True)
-    opposite = me.at(other_z=True)
+    load_hidden = pltpu.make_async_copy(hid_hbm, hid, local.at[0])
+    load_queries = pltpu.make_async_copy(q_hbm, q, local.at[1])
+    load_hidden.start()
+    load_queries.start()
 
     def peer(distance):
         return (wrap(me.s + distance, owners), me.f)
@@ -258,36 +302,26 @@
         for other in others:
             pl.semaphore_signal(barrier, inc=1, device_id=other, device_id_type=MESH)
         lax.fori_loop(1, owners, greet, 0)
+        pl.semaphore_wait(barrier, owners - 1 + len(others))
+        load_hidden.wait()
+
+    def idle():
+        load_queries.wait()
         for h in range(heads):
-            qa[h * BLK : (h + 1) * BLK, 0:HD] = q_ref[:, h * HD : (h + 1) * HD]
+            qa[h * BLK : (h + 1) * BLK, 0:HD] = q[:, h * HD : (h + 1) * HD]
             qa[h * BLK : (h + 1) * BLK, HD : 2 * HD] = qseg_ref[...]
         m_ref[...] = jnp.full_like(m_ref, NEGATIVE)
         l_ref[...] = jnp.zeros_like(l_ref)
         acc_ref[...] = jnp.zeros_like(acc_ref)
-        pl.semaphore_wait(barrier, owners - 1 + len(others))
-
-    finish = project_part(
-        me, hid_ref, gain_ref, w_ref, first_ref, nb, wb, fb, proj, res, got, ass, ars, enter
+
+    finish, opposite_arrived = project_part(
+        me, hid, gain_ref, w_ref, first_ref, qseg_ref, freq_ref,
+        nb, wb, fb, proj, res, begins, buf, ass, ars, local.at[2], enter, idle,
     )
-
     bounds = fb[11]
     low = bounds[0:1, :]
     high = bounds[1:2, :]
-    begin = jnp.sum(
-        qseg_ref[...].astype(jnp.float32) * low.astype(jnp.float32), axis=1, keepdims=True
-    )
-    token = (me.s * BLK + lax.broadcasted_iota(jnp.int32, (BLK, HD), 0)).astype(jnp.float32)
-    angle = (token - begin) * freq_ref[0:1, :]
-    lane = lax.broadcasted_iota(jnp.int32, (BLK, HD), 1)
-    sine = jnp.sin(angle)
-    sine = jnp.where(lane < HD // 2, -sine, sine)
-    projected = got[...].reshape(BLK, 2 * HD)
-    keys = projected[:, 0:HD]
-    swapped = jnp.concatenate([keys[:, HD // 2 :], keys[:, : HD // 2]], axis=1)
-    turned = keys * jnp.cos(angle) + swapped * sine
-    kv = jnp.concatenate([turned, projected[:, HD:]], axis=1).astype(jnp.bfloat16)
     kv_ref = buf.at[0, 0, z, c]
-    kv_ref[...] = kv
 
     def send(index, src, dst, target):
         remote(src, dst, ss.at[index], rs.at[index], target).start()
@@ -337,7 +371,7 @@
         (0, 0, 0, None, 0),
         (0, 1, 0, 3, 7),
         (0, 2, 0, 5, 9),
-        (0, 0, 1, 1, 2),
+        (0, 0, 1, None, 2),
         (0, 1, 1, 4, 8),
         (0, 2, 1, 6, 10),
     ]
@@ -348,12 +382,11 @@
     units = [units[i] for i in turn]
 
     send(0, kv_ref, block(0, 0, 0, c), core)
-    send(1, kv_ref, block(0, 0, 0, c), opposite)
     send_y(0)
 
     row = lax.broadcasted_iota(jnp.int32, (owners * 8, BLK), 0)
     select = (row == target_ref[0:1, :]).astype(jnp.bfloat16)
-    chosen_pages = jnp.dot(select, kv, preferred_element_type=jnp.float32)
+    chosen_pages = jnp.dot(select, kv_ref[...], preferred_element_type=jnp.float32)
     pages_ref[...] = chosen_pages.astype(jnp.bfloat16).reshape(pages_ref.shape)
     pages[me.s] = pages_ref[me.s]
 
@@ -394,7 +427,11 @@
 
     def serve(i):
         rx, k, zi, first, then = units[i]
-        forward(first, then, rx, k, zi)
+        if first is None:
+            opposite_arrived()
+            send(then, mine(rx, k, zi), mine(rx, k, zi), core)
+        else:
+            forward(first, then, rx, k, zi)
         if (rx, k) == (0, 1):
             send_first(zi)
         if (rx, k) == (0, 2):
@@ -453,7 +490,7 @@
     exchange.wait_recv()
     cache_ref[...] = pages[...]
     exchange.wait_send()
-    for index in range(35):
+    for index in [0] + list(range(2, 35)):
         remote(kv_ref, block(0, 0, 0, c), ss.at[index], rs.at[index], core).wait_send()
     finish()
 
@@ -463,6 +500,7 @@
     rows, width = hidden.shape
     columns = weight.shape[1]
     owners = lax.axis_size("seq")
+    away = pl.BlockSpec(memory_space=pl.ANY)
     vmem = pl.BlockSpec(memory_space=pltpu.VMEM)
     return pl.pallas_call(
         layer_kernel,
@@ -470,17 +508,20 @@
             jax.ShapeDtypeStruct(queries.shape, jnp.bfloat16),
             jax.ShapeDtypeStruct((owners, 8, columns), jnp.bfloat16),
         ),
-        in_specs=[vmem] * 8,
+        in_specs=[away, vmem, away, vmem, away, vmem, vmem, vmem],
         out_specs=(vmem, vmem),
         scratch_shapes=[
+            pltpu.VMEM(hidden.shape, jnp.bfloat16),
+            pltpu.VMEM(queries.shape, jnp.bfloat16),
             pltpu.VMEM((2, 2, 4, rows, width // 4), jnp.bfloat16),
             pltpu.VMEM((16, 2, width // 32, columns), jnp.bfloat16),
             pltpu.VMEM((12, 8, HD), jnp.int32),
             pltpu.VMEM((4 * rows, columns), jnp.float32),
-            pltpu.VMEM((2, 2 * rows, columns), jnp.float32),
-            pltpu.VMEM((2, 2 * rows, columns), jnp.float32),
-            pltpu.SemaphoreType.DMA((57,)),
-            pltpu.SemaphoreType.DMA((57,)),
+            pltpu.VMEM((2, 2 * rows, columns), jnp.bfloat16),
+            pltpu.VMEM((2, 4 * rows, HD), jnp.float32),
+            pltpu.SemaphoreType.DMA((60,)),
+            pltpu.SemaphoreType.DMA((60,)),
+            pltpu.SemaphoreType.DMA((3,)),
             pltpu.VMEM((4, 3, 2, 2, BLK, 2 * HD), jnp.bfloat16),
             pltpu.VMEM((owners, 8, columns), jnp.bfloat16),
             pltpu.VMEM((owners, 8, columns), jnp.bfloat16),

time: 117 us -> 118 us (level)
  the two profiles are of different devices: /device:TPU:57 before, /device:TPU:49 now
where the time goes in v5:
time: 118 us; the launch traced here: 117 us
  Pallas kernels  111 us (94%)
  local copies, waits for them, and re-layouts  4.76 us (4%)
    pallas_call x1, Pallas kernels, layer(): pl.pallas_call(layer_kernel, out_shape=(jax.ShapeDtypeStruct(queries.shap...  111 us
    unnamed x11, local copies, waits for them, and re-layouts  3.85 us

profile of v5, /device:TPU:49, one launch (start us, length us, event | category | flops | bytes accessed | tf_op | source)
XLA Modules:
  0.0 117.0 jit_solution(14005879555609434453)
XLA Ops:
  0.6 0.0 copy-start.4
  0.6 0.6 copy-done.4
  1.3 0.2 convert_reduce_fusion
  1.5 0.1 pad_maximum_fusion
  1.6 0.0 copy-start.3
  1.6 0.7 copy-done.3
  2.3 0.2 select_reduce_fusion
  2.5 0.1 iota_add_fusion
  2.6 0.0 copy-start.2
  2.6 0.1 add.60
  2.7 0.0 copy-start.1
  2.7 0.6 copy-done.2
  3.3 0.1 fusion.qseg_ref
  3.4 0.1 copy-done.1
  3.5 0.0 copy-start
  3.5 1.0 copy-done
  4.6 110.9 %shard_map.77 = (bf16[256,1024]{1,0:T(8,128)(2,1)S(1)}, bf16[64,8,256]{2,1,0:T(8,128)(2,1)S(1)}) custom-call(bf16[64,8192]{1,0:T(8,128)(2,1)} %hid_hbm.1, bf16[1,8192]{1,0:T(2,128)(2,1)S(1)} %broadcast_in_dim.18.gain_ref, bf16[128,256]{1,0:T(8,128)(2,1)S(1)} %copy-done.1, s32[8,128]{1,0:T(8,128)S(1)} %pad.4.first_ref, bf16[256,1024]{1,0:T(8,128)(2,1)S(1)} %copy-done, ...), custom_call_target="tpu_custom_call" | custom-call | flops 10000000000 | bytes 4000000 | tf_op jit(solution)/shard_map/pallas_call | solution.py:505
  115.4 0.8 reshape.39
  116.2 0.8 copy.9
  (10 shorter events, 0.1 us)
Async XLA Ops:
  0.6 0.7 copy-start.4
  1.6 0.7 copy-start.3
  2.6 0.7 copy-start.2
  2.7 0.8 copy-start.1
  3.5 1.0 copy-start

commit v6 on v5

--- a/solution.py
+++ b/solution.py
@@ -378,7 +378,7 @@
     for zi in (0, 1):
         units += [(rx, 1 - in_wrap[rx], zi, x1(rx, zi), x1(rx, zi) + 12) for rx in order]
         units += [(rx, in_wrap[rx], zi, x2(rx, zi), x2(rx, zi) + 12) for rx in order]
-    turn = [0, 1, 2, 3, 6, 7, 8, 4, 5, 9, 10, 11, 12, 13, 14, 15, 16, 17]
+    turn = [0, 3, 1, 2, 4, 5, 6, 7, 8, 9, 10, 11, 12, 13, 14, 15, 16, 17]
     units = [units[i] for i in turn]
 
     send(0, kv_ref, block(0, 0, 0, c), core)

time: 118 us -> 116 us (0.983)
  no operation moved by 1% of the time
where the time goes in v6:
time: 116 us
  Pallas kernels  110 us (95%)
  local copies, waits for them, and re-layouts  4.76 us (4%)
    pallas_call x1, Pallas kernels, layer(): pl.pallas_call(layer_kernel, out_shape=(jax.ShapeDtypeStruct(queries.shap...  110 us
    unnamed x11, local copies, waits for them, and re-layouts  3.85 us

profile of v6, /device:TPU:49, one launch (start us, length us, event | category | flops | bytes accessed | tf_op | source)
XLA Modules:
  0.0 116.1 jit_solution(4789142215234909230)
XLA Ops:
  0.6 0.0 copy-start.4
  0.6 0.6 copy-done.4
  1.3 0.2 convert_reduce_fusion
  1.5 0.1 pad_maximum_fusion
  1.6 0.0 copy-start.3
  1.6 0.7 copy-done.3
  2.3 0.2 select_reduce_fusion
  2.5 0.1 iota_add_fusion
  2.6 0.0 copy-start.2
  2.6 0.1 add.60
  2.7 0.0 copy-start.1
  2.7 0.6 copy-done.2
  3.3 0.1 fusion.qseg_ref
  3.4 0.1 copy-done.1
  3.5 0.0 copy-start
  3.5 1.0 copy-done
  4.6 110.0 %shard_map.77 = (bf16[256,1024]{1,0:T(8,128)(2,1)S(1)}, bf16[64,8,256]{2,1,0:T(8,128)(2,1)S(1)}) custom-call(bf16[64,8192]{1,0:T(8,128)(2,1)} %hid_hbm.1, bf16[1,8192]{1,0:T(2,128)(2,1)S(1)} %broadcast_in_dim.18.gain_ref, bf16[128,256]{1,0:T(8,128)(2,1)S(1)} %copy-done.1, s32[8,128]{1,0:T(8,128)S(1)} %pad.4.first_ref, bf16[256,1024]{1,0:T(8,128)(2,1)S(1)} %copy-done, ...), custom_call_target="tpu_custom_call" | custom-call | flops 10000000000 | bytes 4000000 | tf_op jit(solution)/shard_map/pallas_call | solution.py:505
  114.5 0.8 reshape.39
  115.3 0.8 copy.9
  (10 shorter events, 0.1 us)
Async XLA Ops:
  0.6 0.7 copy-start.4
  1.6 0.7 copy-start.3
  2.6 0.7 copy-start.2
  2.7 0.8 copy-start.1
  3.5 1.0 copy-start

commit v7 on v6

--- a/solution.py
+++ b/solution.py
@@ -128,26 +128,47 @@
     back = lambda v, k: lax.rem(v + 4 - k, 4)
     order = (1, 3, 2)
     seed_arrived(0)
-    for k in order:
+    for k in (1, 3):
         send(24 + k, half(y, x, 0), half(y, x, 0), ring_x[k])
     seed_arrived(1)
-    for k in order:
+    for k in (1, 3):
         send(27 + k, half(y, x, 1), half(y, x, 1), ring_y[k])
 
     a2 = lambda k, j: 31 + (k - 1) * 4 + j
     b2 = lambda k, j: 43 + (k - 1) * 4 + j
+
+    cut = wb.shape[2] // 2
+    lower = lambda yy, xx, hh: wb.at[yy * 4 + xx, hh, 0:cut]
+    upper = lambda yy, xx, hh: wb.at[yy * 4 + xx, hh, cut : 2 * cut]
 
     def spread(j):
         ya, xa = y, back(x, j)
         yb, xb = back(y, j), x
-        if j:
-            arrived(24 + j, half(ya, xa, 0))
-        for k in order:
+        for k in (1, 3):
             send(a2(k, j), half(ya, xa, 0), half(ya, xa, 0), ring_y[k])
-        if j:
-            arrived(27 + j, half(yb, xb, 1))
-        for k in order:
             send(b2(k, j), half(yb, xb, 1), half(yb, xb, 1), ring_x[k])
+
+    def pass_on(firsts, halves, near_by, ring):
+        arrived(firsts[0], half(*near_by(1)))
+        send(halves[0], lower(*near_by(1)), lower(*near_by(1)), ring[1])
+        arrived(firsts[1], half(*near_by(3)))
+        send(halves[1], upper(*near_by(3)), upper(*near_by(3)), ring[3])
+
+    def far_arrived(halves, at):
+        arrived(halves[0], lower(*at))
+        arrived(halves[1], upper(*at))
+
+    def relay_first():
+        pass_on((25, 27), (26, 60), lambda k: (y, back(x, k), 0), ring_x)
+        pass_on((28, 30), (29, 61), lambda k: (back(y, k), x, 1), ring_y)
+
+    def relay(j):
+        pass_on(
+            (a2(1, j), a2(3, j)), (a2(2, j), 62 + j), lambda k: (back(y, k), back(x, j), 0), ring_y
+        )
+        pass_on(
+            (b2(1, j), b2(3, j)), (b2(2, j), 66 + j), lambda k: (back(y, j), back(x, k), 1), ring_x
+        )
 
     def forward(i):
         arrived(13 + i, nb.at[c, 1 - parity, i])
@@ -161,16 +182,23 @@
     for k in order:
         send(6 + k, fb.at[3], fb.at[3 + k], ring_x[k])
     forward(0)
+    relay_first()
     spread(1)
     spread(3)
+    far_arrived((26, 60), (y, back(x, 2), 0))
+    far_arrived((29, 61), (back(y, 2), x, 1))
+    spread(2)
     forward(1)
-    spread(2)
+    relay(0)
     for k in order:
         arrived(6 + k, fb.at[3 + k])
     fb[7] = jnp.minimum(jnp.minimum(fb[3], fb[4]), jnp.minimum(fb[5], fb[6]))
     for k in order:
         send(9 + k, fb.at[7], fb.at[7 + k], ring_y[k])
+    relay(1)
     forward(2)
+    relay(3)
+    relay(2)
     forward(3)
     for k in order:
         arrived(9 + k, fb.at[7 + k])
@@ -195,14 +223,16 @@
     for j in order:
         multiply(y, back(x, j), 0)
         multiply(back(y, j), x, 1)
-    for j in (0, 1, 3, 2):
-        for k in order:
-            yy, xx = back(y, k), back(x, j)
-            arrived(a2(k, j), half(yy, xx, 0))
-            multiply(yy, xx, 0)
-            yy, xx = back(y, j), back(x, k)
-            arrived(b2(k, j), half(yy, xx, 1))
-            multiply(yy, xx, 1)
+    for k in (1, 3, 2):
+        for j in (0, 1, 3, 2):
+            ya, xa = back(y, k), back(x, j)
+            yb, xb = back(y, j), back(x, k)
+            if k == 2:
+                far_arrived((a2(2, j), 62 + j), (ya, xa, 0))
+            multiply(ya, xa, 0)
+            if k == 2:
+                far_arrived((b2(2, j), 66 + j), (yb, xb, 1))
+            multiply(yb, xb, 1)
 
     arrived(59, begins.at[1 - c])
     pair = 2 * rows
@@ -519,8 +549,8 @@
             pltpu.VMEM((4 * rows, columns), jnp.float32),
             pltpu.VMEM((2, 2 * rows, columns), jnp.bfloat16),
             pltpu.VMEM((2, 4 * rows, HD), jnp.float32),
-            pltpu.SemaphoreType.DMA((60,)),
-            pltpu.SemaphoreType.DMA((60,)),
+            pltpu.SemaphoreType.DMA((70,)),
+            pltpu.SemaphoreType.DMA((70,)),
             pltpu.SemaphoreType.DMA((3,)),
             pltpu.VMEM((4, 3, 2, 2, BLK, 2 * HD), jnp.bfloat16),
             pltpu.VMEM((owners, 8, columns), jnp.bfloat16),

time: 116 us -> 111 us (0.957); the launches traced: 116 us -> 110 us
  Pallas kernels: 110 us -> 104 us
    pallas_call x1, Pallas kernels: 110 us -> 104 us  [layer(): pl.pallas_call(layer_kernel, out_shape=(jax.ShapeDtypeStruct(queries.shap...]
where the time goes in v7:
time: 111 us; the launch traced here: 110 us
  Pallas kernels  104 us (94%)
  local copies, waits for them, and re-layouts  4.76 us (4%)
    pallas_call x1, Pallas kernels, layer(): pl.pallas_call(layer_kernel, out_shape=(jax.ShapeDtypeStruct(queries.shap...  104 us
    unnamed x11, local copies, waits for them, and re-layouts  3.85 us

profile of v7, /device:TPU:49, one launch (start us, length us, event | category | flops | bytes accessed | tf_op | source)
XLA Modules:
  0.0 109.9 jit_solution(2575855007793339919)
XLA Ops:
  0.6 0.0 copy-start.4
  0.6 0.6 copy-done.4
  1.3 0.2 convert_reduce_fusion
  1.5 0.1 pad_maximum_fusion
  1.6 0.0 copy-start.3
  1.6 0.7 copy-done.3
  2.3 0.2 select_reduce_fusion
  2.5 0.1 iota_add_fusion
  2.6 0.0 copy-start.2
  2.6 0.1 add.60
  2.7 0.0 copy-start.1
  2.7 0.6 copy-done.2
  3.3 0.1 fusion.qseg_ref
  3.4 0.1 copy-done.1
  3.5 0.0 copy-start
  3.5 1.0 copy-done
  4.6 103.8 %shard_map.77 = (bf16[256,1024]{1,0:T(8,128)(2,1)S(1)}, bf16[64,8,256]{2,1,0:T(8,128)(2,1)S(1)}) custom-call(bf16[64,8192]{1,0:T(8,128)(2,1)} %hid_hbm.1, bf16[1,8192]{1,0:T(2,128)(2,1)S(1)} %broadcast_in_dim.18.gain_ref, bf16[128,256]{1,0:T(8,128)(2,1)S(1)} %copy-done.1, s32[8,128]{1,0:T(8,128)S(1)} %pad.4.first_ref, bf16[256,1024]{1,0:T(8,128)(2,1)S(1)} %copy-done, ...), custom_call_target="tpu_custom_call" | custom-call | flops 10000000000 | bytes 4000000 | tf_op jit(solution)/shard_map/pallas_call | solution.py:535
  108.3 0.8 reshape.39
  109.1 0.8 copy.9
  (10 shorter events, 0.1 us)
Async XLA Ops:
  0.6 0.7 copy-start.4
  1.6 0.7 copy-start.3
  2.6 0.7 copy-start.2
  2.7 0.8 copy-start.1
  3.5 1.0 copy-start

commit v8 on v7

--- a/solution.py
+++ b/solution.py
@@ -436,10 +436,10 @@
             column = lax.broadcasted_iota(jnp.int32, scores.shape, 1)
             scores = jnp.where(column <= row, scores, NEGATIVE)
         old = m_ref[...]
-        new = jnp.maximum(old, jnp.max(scores, axis=1, keepdims=True))
-        offset = new * scale2
-        weights = jnp.exp2(scores * scale2 - jnp.concatenate([offset, offset], axis=1))
-        factor = jnp.exp2((old - new) * scale2)
+        top = jnp.maximum(scores[:, 0:HD], scores[:, HD : 2 * HD])
+        new = jnp.maximum(old, jnp.max(top, axis=1, keepdims=True) * scale2)
+        weights = jnp.exp2(scores * scale2 - jnp.concatenate([new, new], axis=1))
+        factor = jnp.exp2(old - new)
         m_ref[...] = new
         l_ref[...] = l_ref[...] * factor + (weights[:, 0:HD] + weights[:, HD : 2 * HD])
         update = jnp.dot(

time: 111 us -> 110 us (level)
  no operation moved by 1% of the time
where the time goes in v8:
time: 110 us; the launch traced here: 109 us
  Pallas kernels  103 us (94%)
  local copies, waits for them, and re-layouts  4.76 us (4%)
    pallas_call x1, Pallas kernels, layer(): pl.pallas_call(layer_kernel, out_shape=(jax.ShapeDtypeStruct(queries.shap...  103 us
    unnamed x11, local copies, waits for them, and re-layouts  3.85 us

profile of v8, /device:TPU:49, one launch (start us, length us, event | category | flops | bytes accessed | tf_op | source)
XLA Modules:
  0.0 109.0 jit_solution(1124515003118086198)
XLA Ops:
  0.6 0.0 copy-start.4
  0.6 0.6 copy-done.4
  1.3 0.2 convert_reduce_fusion
  1.5 0.1 pad_maximum_fusion
  1.6 0.0 copy-start.3
  1.6 0.7 copy-done.3
  2.3 0.2 select_reduce_fusion
  2.5 0.1 iota_add_fusion
  2.6 0.0 copy-start.2
  2.6 0.1 add.60
  2.7 0.0 copy-start.1
  2.7 0.6 copy-done.2
  3.3 0.1 fusion.qseg_ref
  3.4 0.1 copy-done.1
  3.5 0.0 copy-start
  3.5 1.0 copy-done
  4.6 102.9 %shard_map.77 = (bf16[256,1024]{1,0:T(8,128)(2,1)S(1)}, bf16[64,8,256]{2,1,0:T(8,128)(2,1)S(1)}) custom-call(bf16[64,8192]{1,0:T(8,128)(2,1)} %hid_hbm.1, bf16[1,8192]{1,0:T(2,128)(2,1)S(1)} %broadcast_in_dim.18.gain_ref, bf16[128,256]{1,0:T(8,128)(2,1)S(1)} %copy-done.1, s32[8,128]{1,0:T(8,128)S(1)} %pad.4.first_ref, bf16[256,1024]{1,0:T(8,128)(2,1)S(1)} %copy-done, ...), custom_call_target="tpu_custom_call" | custom-call | flops 10000000000 | bytes 4000000 | tf_op jit(solution)/shard_map/pallas_call | solution.py:535
  107.5 0.8 reshape.39
  108.2 0.8 copy.9
  (10 shorter events, 0.1 us)
Async XLA Ops:
  0.6 0.7 copy-start.4
  1.6 0.7 copy-start.3
  2.6 0.7 copy-start.2
  2.7 0.8 copy-start.1
  3.5 1.0 copy-start

commit v9 on v8

--- a/solution.py
+++ b/solution.py
@@ -410,6 +410,7 @@
         units += [(rx, in_wrap[rx], zi, x2(rx, zi), x2(rx, zi) + 12) for rx in order]
     turn = [0, 3, 1, 2, 4, 5, 6, 7, 8, 9, 10, 11, 12, 13, 14, 15, 16, 17]
     units = [units[i] for i in turn]
+    served_at = [0, 0, 0, 1, 1, 2] + [i - 1 for i in range(6, len(units))]
 
     send(0, kv_ref, block(0, 0, 0, c), core)
     send_y(0)
@@ -472,7 +473,7 @@
     def one_unit(n, carry):
         for i in range(1, len(units)):
 
-            @pl.when(n == i - 1)
+            @pl.when(n == served_at[i])
             def _():
                 serve(i)
 

time: 110 us -> 110 us (level)
  no operation moved by 1% of the time
where the time goes in v9:
time: 110 us; the launch traced here: 109 us
  Pallas kernels  103 us (94%)
  local copies, waits for them, and re-layouts  4.76 us (4%)
    pallas_call x1, Pallas kernels, layer(): pl.pallas_call(layer_kernel, out_shape=(jax.ShapeDtypeStruct(queries.shap...  103 us
    unnamed x11, local copies, waits for them, and re-layouts  3.85 us

profile of v9, /device:TPU:49, one launch (start us, length us, event | category | flops | bytes accessed | tf_op | source)
XLA Modules:
  0.0 109.0 jit_solution(10298110332867191144)
XLA Ops:
  0.6 0.0 copy-start.4
  0.6 0.6 copy-done.4
  1.3 0.2 convert_reduce_fusion
  1.5 0.1 pad_maximum_fusion
  1.6 0.0 copy-start.3
  1.6 0.7 copy-done.3
  2.3 0.2 select_reduce_fusion
  2.5 0.1 iota_add_fusion
  2.6 0.0 copy-start.2
  2.6 0.1 add.60
  2.7 0.0 copy-start.1
  2.7 0.6 copy-done.2
  3.3 0.1 fusion.qseg_ref
  3.4 0.1 copy-done.1
  3.5 0.0 copy-start
  3.5 1.0 copy-done
  4.6 102.9 %shard_map.77 = (bf16[256,1024]{1,0:T(8,128)(2,1)S(1)}, bf16[64,8,256]{2,1,0:T(8,128)(2,1)S(1)}) custom-call(bf16[64,8192]{1,0:T(8,128)(2,1)} %hid_hbm.1, bf16[1,8192]{1,0:T(2,128)(2,1)S(1)} %broadcast_in_dim.18.gain_ref, bf16[128,256]{1,0:T(8,128)(2,1)S(1)} %copy-done.1, s32[8,128]{1,0:T(8,128)S(1)} %pad.4.first_ref, bf16[256,1024]{1,0:T(8,128)(2,1)S(1)} %copy-done, ...), custom_call_target="tpu_custom_call" | custom-call | flops 10000000000 | bytes 4000000 | tf_op jit(solution)/shard_map/pallas_call | solution.py:536
  107.4 0.8 reshape.39
  108.2 0.8 copy.9
  (10 shorter events, 0.1 us)
Async XLA Ops:
  0.6 0.7 copy-start.4
  1.6 0.7 copy-start.3
  2.6 0.7 copy-start.2
  2.7 0.8 copy-start.1
  3.5 1.0 copy-start
